TPU v7x, 32 devices: a whole 2x2x4 slice. The times are simulated.
32 devices in a mesh: seq: 8 (over z, y), head: 4 (over x, core).
Axes of the slice: x: 2, y: 2, z: 4, core: 2. Of those that a mesh axis runs over, the one named last changes fastest.
Arguments:
- layer_input: bfloat16 [1, 1024, 1024], P(None, 'seq'), may hold values from -6 to 6
- first_layer_value: bfloat16 [1, 1024, 1024], P(None, 'seq', 'head'), may hold values from -6 to 6
- cotangent: bfloat16 [1, 1024, 1024], P(None, 'seq'), may hold values from -6 to 6
- receptance_weight: bfloat16 [1024, 1024], P('seq', 'head'), may hold values from -0.1875 to 0.1875
- key_weight: bfloat16 [1024, 1024], P('seq', 'head'), may hold values from -0.1875 to 0.1875
- value_weight: bfloat16 [1024, 1024], P('seq', 'head'), may hold values from -0.1875 to 0.1875
- output_weight: bfloat16 [1024, 1024], P('head', 'seq'), may hold values from -0.375 to 0.375
- channel_key_weight: bfloat16 [1024, 4096], P('seq', 'head'), may hold values from -0.1875 to 0.1875
- channel_value_weight: bfloat16 [4096, 1024], P('head', 'seq'), may hold values from -0.09375 to 0.09375
- decay_second_factor: bfloat16 [64, 1024], P('seq', 'head'), may hold values from -0.1875 to 0.1875
- learn_second_factor: bfloat16 [64, 1024], P('seq', 'head'), may hold values from -0.75 to 0.75
- residual_second_factor: bfloat16 [32, 1024], P('seq', 'head'), may hold values from -1 to 1
- gate_second_factor: bfloat16 [160, 1024], P('seq', 'head'), may hold values from -1 to 1
- decay_first_factor: bfloat16 [1024, 64], P(('seq', 'head')), may hold values from -0.1875 to 0.1875
- learn_first_factor: bfloat16 [1024, 64], P(('seq', 'head')), may hold values from -0.1875 to 0.1875
- residual_first_factor: bfloat16 [1024, 32], P(('seq', 'head')), may hold values from -0.1875 to 0.1875
- gate_first_factor: bfloat16 [1024, 160], P(('seq', 'head')), may hold values from -0.1875 to 0.1875
- vectors: float32 [1024, 19], P(('seq', 'head')), as said below
Outputs:
- result: float32 [1, 1024, 1024], P(None, 'seq', 'head')
- d_x_in: float32 [1, 1024, 1024], P(None, 'seq', 'head')
- d_v_first: float32 [1, 1024, 1024], P(None, 'seq', 'head')
- d_w_recept: float32 [1024, 1024], P('seq', 'head')
- d_w_key: float32 [1024, 1024], P('seq', 'head')
- d_w_value: float32 [1024, 1024], P('seq', 'head')
- d_w_out: float32 [1024, 1024], P('head', 'seq')
- d_w_ffn_key: float32 [1024, 4096], P('seq', 'head')
- d_w_ffn_value: float32 [4096, 1024], P('head', 'seq')
- d_lora_b_decay: float32 [64, 1024], P('seq', 'head')
- d_lora_b_iclr: float32 [64, 1024], P('seq', 'head')
- d_lora_b_mix: float32 [32, 1024], P('seq', 'head')
- d_lora_b_gate: float32 [160, 1024], P('seq', 'head')
- d_lora_a_decay: float32 [1024, 64], P(('seq', 'head'))
- d_lora_a_iclr: float32 [1024, 64], P(('seq', 'head'))
- d_lora_a_mix: float32 [1024, 32], P(('seq', 'head'))
- d_lora_a_gate: float32 [1024, 160], P(('seq', 'head'))
- d_vectors: float32 [1024, 19], P(('seq', 'head'))
Inputs may be any that keep to these rules, and one draw needn't show every extreme that they name: Column c of vectors is one per-channel vector: 0 and 1 the first LayerNorm's gain (0.5 to 1.5) and bias (-0.5 to 0.5); 2 to 7 the token-shift mixes of receptance, decay, key, value, learning rate and gate (0 to 1); 8 the decay offset (log(0.3 / 1024) to 0); 9 the learning-rate offset (log(1 / 1024) to 1); 10 the value-residual offset (-1 to 1); 11 a key scaling (0.5 to 1.5); 12 a key scaling (0 to 1); 13 the bonus weights (-1 to 1); 14 and 15 the GroupNorm's gain and bias; 16 and 17 the second LayerNorm's gain and bias (ranges as for 0 and 1); 18 the channel mix's token-shift mix (0 to 1).
All inputs are finite; a program needn't handle non-finite values.
Results may differ from a plain program's by a relative error of at most 0.023.
Values may be sent and summed in bfloat16 or wider, within the bound.
No kernel may reach another device: no remote copies, remote signals or barrier semaphores. Data moves between devices by JAX's collectives and lax.ppermute only.
A program may use at most 128 MiB of HBM per device.

v0:
```python
import jax
import jax.numpy as jnp
from jax import lax
from jax.sharding import PartitionSpec as P

HEAD = 64


NORM_EPS = 1e-05
GROUP_EPS = 0.00064
UNIT_EPS = 1e-06
DECAY_SCALE = 0.606531
HIGHEST = lax.Precision.HIGHEST


def from_behind(block, axis, distance):
    devices = range(lax.axis_size(axis))
    route = [(i - distance, i) for i in devices if i - distance in devices]
    return lax.ppermute(block, axis, route)


def carried_in(value, axis, combine, identity):
    length, place = (lax.axis_size(axis), lax.axis_index(axis))
    everything = jax.tree.map(
        lambda part, kind: lax.all_gather(part.astype(kind), axis),
        value,
        jax.tree.map(lambda a: jnp.bfloat16 if a.dtype == jnp.float32 else a.dtype, value),
    )
    start = jax.tree.map(
        lambda part, zero: jnp.broadcast_to(jnp.asarray(zero, part.dtype), part.shape),
        value,
        identity,
    )

    def hop(k, before):
        reached = k < place
        new = combine(
            before, jax.tree.map(lambda part, own: part[k].astype(own.dtype), everything, value)
        )
        return jax.tree.map(lambda a, b: jnp.where(reached, a, b), new, before)

    return lax.fori_loop(0, length, hop, start)


def carried_in_2(value, axis, combine, identity):
    length, place = (lax.axis_size(axis), lax.axis_index(axis))
    everything = jax.tree.map(
        lambda part, kind: lax.all_gather(part.astype(kind), axis),
        value,
        (jnp.bfloat16, jnp.bfloat16),
    )
    start = jax.tree.map(
        lambda part, zero: jnp.broadcast_to(jnp.asarray(zero, part.dtype), part.shape),
        value,
        identity,
    )

    def hop(k, before):
        at = length - 1 - k
        reached = at > place
        new = combine(
            before, jax.tree.map(lambda part, own: part[at].astype(own.dtype), everything, value)
        )
        return jax.tree.map(lambda a, b: jnp.where(reached, a, b), new, before)

    return lax.fori_loop(0, length, hop, start)


def narrow_dot(former, latter):
    return jnp.dot(
        former.astype(jnp.bfloat16), latter.astype(jnp.bfloat16), preferred_element_type=jnp.float32
    )


def narrow_tn(former, latter):
    return lax.dot_general(
        former.astype(jnp.bfloat16),
        latter.astype(jnp.bfloat16),
        (((0,), (0,)), ((), ())),
        preferred_element_type=jnp.float32,
    )


def narrow_nt(former, latter):
    return lax.dot_general(
        former.astype(jnp.bfloat16),
        latter,
        (((1,), (1,)), ((), ())),
        preferred_element_type=jnp.float32,
    )


def exact_tn(former, latter):
    return lax.dot_general(former, latter, (((0,), (0,)), ((), ())), precision=HIGHEST)


def exact_nt(former, latter):
    return lax.dot_general(former, latter, (((1,), (1,)), ((), ())), precision=HIGHEST)


def exact_ein(pattern, former, latter):
    return jnp.einsum(pattern, former, latter, precision=HIGHEST)


def layer_norm(values, gain_column, bias_column):
    average = jnp.mean(values, axis=-1, keepdims=True)
    centred = values - average
    spread = jnp.mean(centred * centred, axis=-1, keepdims=True)
    return centred * lax.rsqrt(spread + NORM_EPS) * gain_column + bias_column


def first_norm(values, vectors):
    return layer_norm(values, vectors[:, 0], vectors[:, 1])


def second_norm(values, vectors):
    return layer_norm(values, vectors[:, 16], vectors[:, 17])


def shift_mix(standardized_signal, previous, weights):
    shifted = jnp.concatenate([previous[..., None, :], standardized_signal[..., :-1, :]], axis=-2)
    difference = shifted - standardized_signal
    return tuple(
        (
            standardized_signal + difference * weights[:, column]
            for column in range(weights.shape[1])
        )
    )


def time_inputs(standardized_signal, previous, vectors):
    return shift_mix(standardized_signal, previous, vectors[:, 2:8])


def ffn_inputs(standardized_signal, previous, vectors):
    return shift_mix(standardized_signal, previous, vectors[:, 18:19])[0]


def head_params(
    key_raw, value_raw, decay_shift, learn_shift, mix_shift, first_value, feedforward_sublevel
):
    decays = jnp.exp(-DECAY_SCALE * jax.nn.sigmoid(feedforward_sublevel[:, 8] + decay_shift))
    learn_rate = jax.nn.sigmoid(feedforward_sublevel[:, 9] + learn_shift)
    content_shift_portion = value_raw + (first_value - value_raw) * jax.nn.sigmoid(
        feedforward_sublevel[:, 10] + mix_shift
    )
    scaled = key_raw * feedforward_sublevel[:, 11]
    parameter_arrangement = scaled.shape
    grouped = scaled.reshape(parameter_arrangement[:-1] + (parameter_arrangement[-1] // HEAD, HEAD))
    unit_keys = (
        grouped * lax.rsqrt(jnp.sum(grouped * grouped, axis=-1, keepdims=True) + UNIT_EPS)
    ).reshape(parameter_arrangement)
    lookup_shift_portion = key_raw * (1.0 + (learn_rate - 1.0) * feedforward_sublevel[:, 12])
    return (decays, lookup_shift_portion, content_shift_portion, -unit_keys, unit_keys * learn_rate)


def head_output(
    memory_out,
    acceptance_matrix_lines,
    lookup_shift_portion,
    content_shift_portion,
    gates,
    feedforward_sublevel,
):
    parameter_arrangement = memory_out.shape
    partition_sizes_list = parameter_arrangement[:-1] + (parameter_arrangement[-1] // HEAD, HEAD)
    grouped = memory_out.reshape(partition_sizes_list)
    average = jnp.mean(grouped, axis=-1, keepdims=True)
    centred = grouped - average
    spread = jnp.mean(centred * centred, axis=-1, keepdims=True)
    standardized_signal = (centred * lax.rsqrt(spread + GROUP_EPS)).reshape(
        parameter_arrangement
    ) * feedforward_sublevel[:, 14] + feedforward_sublevel[:, 15]
    current_token_extra = jnp.sum(
        (acceptance_matrix_lines * lookup_shift_portion * feedforward_sublevel[:, 13]).reshape(
            partition_sizes_list
        ),
        axis=-1,
        keepdims=True,
    )
    standardized_signal = standardized_signal + (
        current_token_extra * content_shift_portion.reshape(partition_sizes_list)
    ).reshape(parameter_arrangement)
    return standardized_signal * gates


def to_blocks(member, sequences, head_count, block_len):
    rows = member.shape[0]
    tokens = rows // sequences
    block_count = tokens // block_len
    return (
        member.reshape(sequences, block_count, block_len, head_count, HEAD)
        .transpose(0, 3, 1, 2, 4)
        .reshape(sequences * head_count, block_count, block_len, HEAD)
    )


def from_blocks(member, sequences, head_count):
    batches, block_count, block_len, width = member.shape
    return (
        member.reshape(sequences, head_count, block_count, block_len, width)
        .transpose(0, 2, 3, 1, 4)
        .reshape(sequences * block_count * block_len, head_count * width)
    )


def block_pieces(members):
    (
        decays,
        remover,
        refill,
        lookup_shift_portion,
        content_shift_portion,
        acceptance_matrix_lines,
    ) = members
    block_len = decays.shape[2]
    log_decay = jnp.log(decays)
    inclusive = jnp.cumsum(log_decay, axis=2)
    exclusive = inclusive - log_decay
    ending = inclusive[:, :, -1:, :]
    grow_back = jnp.exp(-inclusive)
    remove_hat = remover * jnp.exp(exclusive)
    refill_inv = refill * grow_back
    key_inv = lookup_shift_portion * grow_back
    recept_hat = acceptance_matrix_lines * jnp.exp(inclusive)
    to_end = jnp.exp(ending - inclusive)
    strict_mask = jnp.tril(jnp.ones((block_len, block_len), jnp.float32), -1)
    inclusive_mask = jnp.tril(jnp.ones((block_len, block_len), jnp.float32))
    refill_pairs = exact_ein("bntk,bnsk->bnts", remove_hat, refill_inv) * strict_mask
    key_pairs = exact_ein("bntk,bnsk->bnts", remove_hat, key_inv) * strict_mask
    read_refill = exact_ein("bntk,bnsk->bnts", recept_hat, refill_inv) * inclusive_mask
    read_key = exact_ein("bntk,bnsk->bnts", recept_hat, key_inv) * inclusive_mask
    unit_eye = jnp.eye(block_len, dtype=jnp.float32)
    inverse = unit_eye + refill_pairs
    powered = refill_pairs
    reach = 2
    while reach < block_len:
        powered = exact_ein("bnts,bnsu->bntu", powered, powered)
        inverse = exact_ein("bnts,bnsu->bntu", inverse, unit_eye + powered)
        reach = reach * 2
    right_sides = jnp.concatenate(
        [exact_ein("bnts,bnsv->bntv", key_pairs, content_shift_portion), remove_hat], axis=-1
    )
    solved = exact_ein("bnts,bnsk->bntk", inverse, right_sides)
    base_along = solved[..., :HEAD]
    along_map = solved[..., HEAD:]
    refill_end = refill * to_end
    key_end = lookup_shift_portion * to_end
    carry_scale = jnp.exp(ending[:, :, 0, :])
    transition = carry_scale[..., :, None] * jnp.eye(HEAD, dtype=jnp.float32) + exact_ein(
        "bnck,bncj->bnkj", along_map, refill_end
    )
    fresh = exact_ein("bncv,bnck->bnvk", base_along, refill_end) + exact_ein(
        "bncv,bnck->bnvk", content_shift_portion, key_end
    )
    reader = recept_hat + exact_ein("bnts,bnsk->bntk", read_refill, along_map)
    base_out = exact_ein("bnts,bnsv->bntv", read_refill, base_along) + exact_ein(
        "bnts,bnsv->bntv", read_key, content_shift_portion
    )
    return (transition, fresh, reader, base_out)


def block_summary(transition, fresh, zero_state, identity):

    def advance(carried, inputs):
        return (
            (
                exact_ein("bvk,bkj->bvj", carried[0], inputs[0]) + inputs[1],
                exact_ein("bvk,bkj->bvj", carried[1], inputs[0]),
            ),
            None,
        )

    carried, _ = lax.scan(
        advance,
        (zero_state, identity),
        (transition.transpose(1, 0, 2, 3), fresh.transpose(1, 0, 2, 3)),
    )
    return carried


def block_starts(initial, transition, fresh):

    def advance(state, inputs):
        return (exact_ein("bvk,bkj->bvj", state, inputs[0]) + inputs[1], state)

    _, starts = lax.scan(
        advance, initial, (transition.transpose(1, 0, 2, 3), fresh.transpose(1, 0, 2, 3))
    )
    return starts.transpose(1, 0, 2, 3)


def block_grads(init_grad, transition, reader, out_grad):

    def retreat(grad_next, inputs):
        grad_start = exact_ein("bvj,bkj->bvk", grad_next, inputs[0]) + exact_ein(
            "bcv,bck->bvk", inputs[2], inputs[1]
        )
        return (grad_start, grad_next)

    carried, later = lax.scan(
        retreat,
        init_grad,
        (
            transition.transpose(1, 0, 2, 3),
            reader.transpose(1, 0, 2, 3),
            out_grad.transpose(1, 0, 2, 3),
        ),
        reverse=True,
    )
    return (carried, later.transpose(1, 0, 2, 3))


def join_forward(earlier, latter):
    return (
        jnp.einsum("bij,bjk->bik", earlier[0], latter[1], precision=HIGHEST) + latter[0],
        jnp.einsum("bij,bjk->bik", earlier[1], latter[1], precision=HIGHEST),
    )


def join_backward(earlier, latter):
    return (
        latter[0] + jnp.einsum("bvk,bjk->bvj", earlier[0], latter[1], precision=HIGHEST),
        jnp.einsum("bij,bjk->bik", latter[1], earlier[1], precision=HIGHEST),
    )


def fetch_weights(shards):
    return (
        lax.all_gather(shards[0], "seq", axis=0, tiled=True),
        lax.all_gather(shards[1], "seq", axis=0, tiled=True),
        lax.all_gather(shards[2], "seq", axis=0, tiled=True),
        lax.all_gather(shards[3], "seq", axis=1, tiled=True),
        lax.all_gather(shards[4], "seq", axis=0, tiled=True),
        lax.all_gather(shards[5], "seq", axis=1, tiled=True),
        lax.all_gather(shards[6], "seq", axis=0, tiled=True),
        lax.all_gather(shards[7], "seq", axis=0, tiled=True),
        lax.all_gather(shards[8], "seq", axis=0, tiled=True),
        lax.all_gather(shards[9], "seq", axis=0, tiled=True),
    )


def pass_last(standardized_signal):
    return from_behind(standardized_signal[:, -1, :], "seq", 1)


def pass_first(grad_rows):
    return from_behind(grad_rows, "seq", -1)


def head_reduce(partial_value):
    return lax.psum_scatter(
        partial_value.astype(jnp.bfloat16), "head", scatter_dimension=1, tiled=True
    ).astype(jnp.float32)


def body(
    layer_input,
    first_layer_value,
    cotangent,
    receptance_weight,
    key_weight,
    value_weight,
    output_weight,
    channel_key_weight,
    channel_value_weight,
    decay_second_factor,
    learn_second_factor,
    residual_second_factor,
    gate_second_factor,
    decay_first_factor,
    learn_first_factor,
    residual_first_factor,
    gate_first_factor,
    vectors,
):
    sequences, tokens, features = layer_input.shape
    channels = first_layer_value.shape[2]
    head_count = channels // HEAD
    row_count = sequences * tokens
    batches = sequences * head_count
    block_len = max(min(tokens, 16), tokens // 16)
    offset = lax.axis_index("head") * channels
    shards = (
        receptance_weight,
        key_weight,
        value_weight,
        output_weight,
        channel_key_weight,
        channel_value_weight,
        decay_second_factor,
        learn_second_factor,
        residual_second_factor,
        gate_second_factor,
    )
    gathered = fetch_weights(shards)
    (
        recept_cols,
        key_cols,
        value_cols,
        out_rows,
        ffn_key_cols,
        ffn_value_rows,
        decay_up,
        learn_up,
        mix_up,
        gate_up,
    ) = gathered
    decay_down, learn_down, mix_down, gate_down, whole_vec = (
        lax.all_gather(decay_first_factor.astype(jnp.float32), ("seq", "head"), axis=0, tiled=True),
        lax.all_gather(learn_first_factor.astype(jnp.float32), ("seq", "head"), axis=0, tiled=True),
        lax.all_gather(
            residual_first_factor.astype(jnp.float32), ("seq", "head"), axis=0, tiled=True
        ),
        lax.all_gather(gate_first_factor.astype(jnp.float32), ("seq", "head"), axis=0, tiled=True),
        lax.all_gather(vectors, ("seq", "head"), axis=0, tiled=True),
    )
    feedforward_sublevel = lax.dynamic_slice_in_dim(whole_vec, offset, channels, 0)
    x_full = layer_input.astype(jnp.float32)
    normed_a = first_norm(x_full, whole_vec)
    prev_a = pass_last(normed_a)
    mixed_recept, mixed_decay, mixed_key, mixed_value, mixed_learn, mixed_gate = [
        member.reshape(row_count, features) for member in time_inputs(normed_a, prev_a, whole_vec)
    ]
    acceptance_matrix_lines = narrow_dot(mixed_recept, recept_cols)
    key_raw = narrow_dot(mixed_key, key_cols)
    value_raw = narrow_dot(mixed_value, value_cols)
    decay_low = narrow_dot(mixed_decay, decay_down)
    learn_low = narrow_dot(mixed_learn, learn_down)
    mix_low = narrow_dot(mixed_value, mix_down)
    gate_low = narrow_dot(mixed_gate, gate_down)
    decay_tanh = jnp.tanh(decay_low)
    gate_sigm = jax.nn.sigmoid(gate_low)
    decay_shift = narrow_dot(decay_tanh, decay_up)
    learn_shift = narrow_dot(learn_low, learn_up)
    mix_shift = narrow_dot(mix_low, mix_up)
    gates = narrow_dot(gate_sigm, gate_up)
    first_value = first_layer_value.astype(jnp.float32).reshape(row_count, channels)
    decays, lookup_shift_portion, content_shift_portion, remover, refill = head_params(
        key_raw, value_raw, decay_shift, learn_shift, mix_shift, first_value, feedforward_sublevel
    )
    members = tuple(
        (
            to_blocks(member, sequences, head_count, block_len)
            for member in (
                decays,
                remover,
                refill,
                lookup_shift_portion,
                content_shift_portion,
                acceptance_matrix_lines,
            )
        )
    )
    pieces, piece_back = jax.vjp(block_pieces, members)
    transition, fresh, reader, base_out = pieces
    zero_state = jnp.zeros((batches, HEAD, HEAD), jnp.float32)
    identity = jnp.broadcast_to(jnp.eye(HEAD, dtype=jnp.float32), (batches, HEAD, HEAD))
    summary = block_summary(transition, fresh, zero_state, identity)
    initial = carried_in(summary, "seq", join_forward, (zero_state, identity))[0]
    starts = block_starts(initial, transition, fresh)
    outputs = exact_ein("bnck,bnvk->bncv", reader, starts) + base_out
    memory_out = from_blocks(outputs, sequences, head_count)
    pre_out = head_output(
        memory_out,
        acceptance_matrix_lines,
        lookup_shift_portion,
        content_shift_portion,
        gates,
        feedforward_sublevel,
    )
    partial_value = narrow_dot(pre_out, out_rows)
    x_rows = x_full.reshape(row_count, features)
    middle = x_rows + lax.psum(partial_value.astype(jnp.bfloat16), "head").astype(jnp.float32)
    middle_seq = middle.reshape(sequences, tokens, features)
    normed_b = second_norm(middle_seq, whole_vec)
    prev_b = pass_last(normed_b)
    mixed_ffn = ffn_inputs(normed_b, prev_b, whole_vec).reshape(row_count, features)
    middle_share = lax.dynamic_slice_in_dim(middle, offset, channels, 1)
    hidden_pre = narrow_dot(mixed_ffn, ffn_key_cols)
    active = jnp.maximum(hidden_pre, 0.0)
    hidden = active * active
    result = middle_share + head_reduce(narrow_dot(hidden, ffn_value_rows))
    gathered = fetch_weights(shards)
    (
        recept_cols,
        key_cols,
        value_cols,
        out_rows,
        ffn_key_cols,
        ffn_value_rows,
        decay_up,
        learn_up,
        mix_up,
        gate_up,
    ) = gathered
    cot_rows = cotangent.reshape(row_count, features)
    grad_ffn_value = narrow_tn(hidden, cot_rows)
    pre_grad = narrow_nt(cot_rows, ffn_value_rows) * 2.0 * active
    grad_ffn_key = narrow_tn(mixed_ffn, pre_grad)
    ffn_back_part = narrow_nt(pre_grad, ffn_key_cols)
    _, ffn_back = jax.vjp(ffn_inputs, normed_b, prev_b, whole_vec)
    normed_b_grad, prev_b_grad, vec_ffn_mix = ffn_back(
        ffn_back_part.reshape(sequences, tokens, features)
    )
    returned_b = pass_first(prev_b_grad)
    normed_b_grad = normed_b_grad.at[:, -1, :].add(returned_b)
    _, norm_b_back = jax.vjp(second_norm, middle_seq, whole_vec)
    middle_part, vec_ffn_norm = norm_b_back(normed_b_grad)
    middle_grad = cot_rows.astype(jnp.float32) + lax.psum(
        middle_part.reshape(row_count, features).astype(jnp.bfloat16), "head"
    ).astype(jnp.float32)
    middle_grad_share = lax.dynamic_slice_in_dim(middle_grad, offset, channels, 1)
    ffn_vec = vec_ffn_mix + vec_ffn_norm
    grad_out = narrow_tn(pre_out, middle_grad)
    pre_out_grad = narrow_nt(middle_grad, out_rows)
    _, output_back = jax.vjp(
        head_output,
        memory_out,
        acceptance_matrix_lines,
        lookup_shift_portion,
        content_shift_portion,
        gates,
        feedforward_sublevel,
    )
    memory_grad, recept_part, key_part, value_part, gate_grad, channel_out = output_back(
        pre_out_grad
    )
    grad_gate_up = narrow_tn(gate_sigm, gate_grad)
    gate_low_grad = narrow_nt(gate_grad, gate_up) * gate_sigm * (1.0 - gate_sigm)
    grad_blocks = to_blocks(memory_grad, sequences, head_count, block_len)
    local_grads, _ = block_grads(zero_state, transition, reader, grad_blocks)
    ending = carried_in_2((local_grads, summary[1]), "seq", join_backward, (zero_state, identity))[
        0
    ]
    _, next_grads = block_grads(ending, transition, reader, grad_blocks)
    transition_grad = exact_ein("bnvj,bnvk->bnjk", starts, next_grads)
    reader_grad = exact_ein("bncv,bnvk->bnck", grad_blocks, starts)
    chain_grads = piece_back((transition_grad, next_grads, reader_grad, grad_blocks))[0]
    decay_grad, remover_grad, refill_grad, key_chain, value_chain, recept_chain = [
        from_blocks(member, sequences, head_count) for member in chain_grads
    ]
    _, param_back = jax.vjp(
        head_params,
        key_raw,
        value_raw,
        decay_shift,
        learn_shift,
        mix_shift,
        first_value,
        feedforward_sublevel,
    )
    (
        key_grad,
        value_grad,
        decay_shift_grad,
        learn_shift_grad,
        mix_shift_grad,
        first_grad,
        channel_param,
    ) = param_back(
        (decay_grad, key_part + key_chain, value_part + value_chain, remover_grad, refill_grad)
    )
    recept_grad = recept_part + recept_chain
    grad_decay_up = narrow_tn(decay_tanh, decay_shift_grad)
    decay_low_grad = narrow_nt(decay_shift_grad, decay_up) * (1.0 - decay_tanh * decay_tanh)
    grad_learn_up = narrow_tn(learn_low, learn_shift_grad)
    learn_low_grad = narrow_nt(learn_shift_grad, learn_up)
    grad_mix_up = narrow_tn(mix_low, mix_shift_grad)
    mix_low_grad = narrow_nt(mix_shift_grad, mix_up)
    grad_decay_down = exact_tn(mixed_decay, decay_low_grad)
    grad_learn_down = exact_tn(mixed_learn, learn_low_grad)
    grad_mix_down = exact_tn(mixed_value, mix_low_grad)
    grad_gate_down = exact_tn(mixed_gate, gate_low_grad)
    grad_recept = narrow_tn(mixed_recept, recept_grad)
    grad_key = narrow_tn(mixed_key, key_grad)
    grad_value = narrow_tn(mixed_value, value_grad)
    mixes_grad = tuple(
        (
            member.reshape(sequences, tokens, features)
            for member in (
                narrow_nt(recept_grad, recept_cols),
                exact_nt(decay_low_grad, decay_down),
                narrow_nt(key_grad, key_cols),
                narrow_nt(value_grad, value_cols) + exact_nt(mix_low_grad, mix_down),
                exact_nt(learn_low_grad, learn_down),
                exact_nt(gate_low_grad, gate_down),
            )
        )
    )
    _, mix_back = jax.vjp(time_inputs, normed_a, prev_a, whole_vec)
    normed_a_grad, prev_a_grad, vec_attn_mix = mix_back(mixes_grad)
    returned_a = pass_first(prev_a_grad)
    normed_a_grad = normed_a_grad.at[:, -1, :].add(returned_a)
    _, norm_a_back = jax.vjp(first_norm, x_full, whole_vec)
    input_part, vec_attn_norm = norm_a_back(normed_a_grad)
    input_grad = middle_grad_share + head_reduce(input_part.reshape(row_count, features))
    vec_grad = (
        ffn_vec
        + vec_attn_mix
        + vec_attn_norm
        + lax.dynamic_update_slice_in_dim(
            jnp.zeros_like(whole_vec), channel_out + channel_param, offset, 0
        )
    )
    big_grads = (
        lax.psum_scatter(
            grad_recept.astype(jnp.bfloat16), "seq", scatter_dimension=0, tiled=True
        ).astype(jnp.float32),
        lax.psum_scatter(
            grad_key.astype(jnp.bfloat16), "seq", scatter_dimension=0, tiled=True
        ).astype(jnp.float32),
        lax.psum_scatter(
            grad_value.astype(jnp.bfloat16), "seq", scatter_dimension=0, tiled=True
        ).astype(jnp.float32),
        lax.psum_scatter(
            grad_out.astype(jnp.bfloat16), "seq", scatter_dimension=1, tiled=True
        ).astype(jnp.float32),
        lax.psum_scatter(
            grad_ffn_key.astype(jnp.bfloat16), "seq", scatter_dimension=0, tiled=True
        ).astype(jnp.float32),
        lax.psum_scatter(
            grad_ffn_value.astype(jnp.bfloat16), "seq", scatter_dimension=1, tiled=True
        ).astype(jnp.float32),
        lax.psum_scatter(
            grad_decay_up.astype(jnp.bfloat16), "seq", scatter_dimension=0, tiled=True
        ).astype(jnp.float32),
        lax.psum_scatter(
            grad_learn_up.astype(jnp.bfloat16), "seq", scatter_dimension=0, tiled=True
        ).astype(jnp.float32),
        lax.psum_scatter(
            grad_mix_up.astype(jnp.bfloat16), "seq", scatter_dimension=0, tiled=True
        ).astype(jnp.float32),
        lax.psum_scatter(
            grad_gate_up.astype(jnp.bfloat16), "seq", scatter_dimension=0, tiled=True
        ).astype(jnp.float32),
    )
    small_grads = (
        lax.psum_scatter(grad_decay_down, ("seq", "head"), scatter_dimension=0, tiled=True),
        lax.psum_scatter(grad_learn_down, ("seq", "head"), scatter_dimension=0, tiled=True),
        lax.psum_scatter(grad_mix_down, ("seq", "head"), scatter_dimension=0, tiled=True),
        lax.psum_scatter(grad_gate_down, ("seq", "head"), scatter_dimension=0, tiled=True),
        lax.psum_scatter(vec_grad, ("seq", "head"), scatter_dimension=0, tiled=True),
    )
    return (
        (
            result.reshape(sequences, tokens, channels),
            input_grad.reshape(sequences, tokens, channels),
            first_grad.reshape(sequences, tokens, channels),
        )
        + tuple(big_grads)
        + tuple(small_grads)
    )


def solution(mesh):
    placed = (
        P(None, "seq", None),
        P(None, "seq", "head"),
        P(None, "seq", None),
        P("seq", "head"),
        P("seq", "head"),
        P("seq", "head"),
        P("head", "seq"),
        P("seq", "head"),
        P("head", "seq"),
        P("seq", "head"),
        P("seq", "head"),
        P("seq", "head"),
        P("seq", "head"),
        P(("seq", "head"), None),
        P(("seq", "head"), None),
        P(("seq", "head"), None),
        P(("seq", "head"), None),
        P(("seq", "head"), None),
    )
    return jax.shard_map(
        body,
        mesh=mesh,
        in_specs=placed,
        out_specs=(
            P(None, "seq", "head"),
            P(None, "seq", "head"),
            P(None, "seq", "head"),
            P("seq", "head"),
            P("seq", "head"),
            P("seq", "head"),
            P("head", "seq"),
            P("seq", "head"),
            P("head", "seq"),
            P("seq", "head"),
            P("seq", "head"),
            P("seq", "head"),
            P("seq", "head"),
            P(("seq", "head"), None),
            P(("seq", "head"), None),
            P(("seq", "head"), None),
            P(("seq", "head"), None),
            P(("seq", "head"), None),
        ),
        check_vma=False,
    )
```

profile of v0, /device:TPU:0, one launch (start us, length us, event | category | flops | bytes accessed | tf_op | source)
XLA Modules:
  0.0 2191.6 jit_solution(5903401939362243363)
XLA Ops:
  8.1 44.7 %all-gather.3 = f32[32,32,19]{1,2,0:T(8,128)S(1)} all-gather(f32[1,32,19]{1,2,0:T(8,128)} %bitcast.767), channel_id=1, replica_groups=mesh['seq'=8,'head'=4] {'seq','head'}, dimensions={0}, use_global_device_ids=true | all-gather | bytes 80256 | tf_op jit(solution)/shard_map/all_gather | solution.py:416
  90.4 37.9 %all_gather.80 = f32[1024,64]{1,0:T(8,128)S(1)} all-gather(f32[32,64]{1,0:T(8,128)S(1)} %convert_element_type.287), channel_id=1, replica_groups=mesh['seq'=8,'head'=4] {'seq','head'}, dimensions={0}, use_global_device_ids=true | all-gather | bytes 270336 | tf_op jit(solution)/shard_map/all_gather | solution.py:411
  128.3 32.2 %all_gather.81 = bf16[64,256]{1,0:T(8,128)(2,1)} all-gather(bf16[8,256]{1,0:T(8,128)(2,1)S(1)} %copy-done.209), channel_id=1, replica_groups=mesh['seq'=8,'head'=4] {'seq'}, dimensions={0}, use_global_device_ids=true | all-gather | bytes 36864 | tf_op jit(solution)/shard_map/all_gather | solution.py:337
  160.5 31.5 %all_gather.76 = bf16[1024,256]{1,0:T(8,128)(2,1)S(1)} all-gather(bf16[128,256]{1,0:T(8,128)(2,1)S(1)} %copy-done.187), channel_id=1, replica_groups=mesh['seq'=8,'head'=4] {'seq'}, dimensions={0}, use_global_device_ids=true | all-gather | bytes 589824 | tf_op jit(solution)/shard_map/all_gather | solution.py:330
  192.0 42.4 %all_gather.83 = f32[1024,32]{1,0:T(8,128)} all-gather(f32[32,32]{1,0:T(8,128)S(1)} %convert_element_type.292), channel_id=1, replica_groups=mesh['seq'=8,'head'=4] {'seq','head'}, dimensions={0}, use_global_device_ids=true | all-gather | bytes 135168 | tf_op jit(solution)/shard_map/all_gather | solution.py:412
  234.4 33.4 %all_gather.82 = bf16[1024,256]{1,0:T(8,128)(2,1)} all-gather(bf16[128,256]{1,0:T(8,128)(2,1)S(1)} %copy-done.188), channel_id=1, replica_groups=mesh['seq'=8,'head'=4] {'seq'}, dimensions={0}, use_global_device_ids=true | all-gather | bytes 589824 | tf_op jit(solution)/shard_map/all_gather | solution.py:332
  267.8 32.1 %all_gather.78 = bf16[64,256]{1,0:T(8,128)(2,1)} all-gather(bf16[8,256]{1,0:T(8,128)(2,1)S(1)} %copy-done.210), channel_id=1, replica_groups=mesh['seq'=8,'head'=4] {'seq'}, dimensions={0}, use_global_device_ids=true | all-gather | bytes 36864 | tf_op jit(solution)/shard_map/all_gather | solution.py:336
  299.9 37.9 %all_gather.77 = f32[1024,64]{1,0:T(8,128)S(1)} all-gather(f32[32,64]{1,0:T(8,128)S(1)} %convert_element_type.281), channel_id=1, replica_groups=mesh['seq'=8,'head'=4] {'seq','head'}, dimensions={0}, use_global_device_ids=true | all-gather | bytes 270336 | tf_op jit(solution)/shard_map/all_gather | solution.py:410
  369.1 43.7 %all_gather.89 = f32[1024,160]{1,0:T(8,128)} all-gather(f32[32,160]{1,0:T(8,128)S(1)} %convert_element_type.299), channel_id=1, replica_groups=mesh['seq'=8,'head'=4] {'seq','head'}, dimensions={0}, use_global_device_ids=true | all-gather | bytes 675840 | tf_op jit(solution)/shard_map/all_gather | solution.py:415
  537.7 31.5 %all-gather = bf16[32,64,64]{2,1,0:T(8,128)(2,1)S(1)} all-gather(bf16[4,64,64]{2,1,0:T(8,128)(2,1)S(1)} %copy.227), channel_id=2, replica_groups=mesh['seq'=8,'head'=4] {'seq'}, dimensions={0}, use_global_device_ids=true | all-gather | bytes 294912 | tf_op jit(solution)/shard_map/all_gather | solution.py:25
  682.8 48.9 %all-gather.11.cloned.1.call-done = bf16[1024,1024]{1,0:T(8,128)(2,1)} async-done(((bf16[1024,128]{1,0:T(8,128)(2,1)}), bf16[1024,1024]{1,0:T(8,128)(2,1)}) %all-gather.11.cloned.1.call-update) | async-done | bytes 2097168 | tf_op jit(solution)/shard_map/all_gather | solution.py:335
  808.4 31.6 %all-gather.2 = bf16[32,64,64]{2,1,0:T(8,128)(2,1)S(1)} all-gather(bf16[4,64,64]{2,1,0:T(8,128)(2,1)S(1)} %copy.245), channel_id=4, replica_groups=mesh['seq'=8,'head'=4] {'seq'}, dimensions={0}, use_global_device_ids=true | all-gather | bytes 294912 | tf_op jit(solution)/shard_map/all_gather | solution.py:48
  1011.9 33.2 %all-reduce.25 = bf16[32,256]{1,0:T(8,128)(2,1)S(1)} all-reduce(bf16[32,256]{1,0:T(8,128)(2,1)S(1)} %convolution_convert_fusion.11), channel_id=15, replica_groups=mesh['seq'=8,'head'=4] {'seq'}, use_global_device_ids=true, to_apply=%region_44.45.clone | all-reduce | flops 8192 | bytes 32768
  1062.2 135.8 %reduce-scatter.52.cloned.1.call-done = f32[32,19]{1,0:T(8,128)} async-done(((f32[1024,19]{1,0:T(8,128)}), f32[32,19]{1,0:T(8,128)}) %reduce-scatter.52.cloned.1.call-update) | async-done | bytes 2448
  1240.2 64.4 %reduce-scatter.48.cloned.1.call-done = bf16[128,256]{1,0:T(8,128)(2,1)} async-done(((bf16[1024,256]{1,0:T(8,128)(2,1)}), bf16[128,256]{1,0:T(8,128)(2,1)}) %reduce-scatter.48.cloned.1.call-update) | async-done | bytes 65552
  1306.3 63.8 %reduce-scatter.28.cloned.1.call-done = bf16[128,256]{1,0:T(8,128)(2,1)} async-done(((bf16[1024,256]{1,0:T(8,128)(2,1)}), bf16[128,256]{1,0:T(8,128)(2,1)}) %reduce-scatter.28.cloned.1.call-update) | async-done | bytes 65552 | tf_op jit(solution)/shard_map/reduce_scatter | solution.py:607
  1371.6 63.6 %reduce-scatter.30.cloned.1.call-done = bf16[128,256]{1,0:T(8,128)(2,1)} async-done(((bf16[1024,256]{1,0:T(8,128)(2,1)}), bf16[128,256]{1,0:T(8,128)(2,1)}) %reduce-scatter.30.cloned.1.call-update) | async-done | bytes 65552 | tf_op jit(solution)/shard_map/reduce_scatter | solution.py:610
  1436.7 63.4 %reduce-scatter.32.cloned.1.call-done = bf16[128,256]{1,0:T(8,128)(2,1)} async-done(((bf16[1024,256]{1,0:T(8,128)(2,1)}), bf16[128,256]{1,0:T(8,128)(2,1)}) %reduce-scatter.32.cloned.1.call-update) | async-done | bytes 65552 | tf_op jit(solution)/shard_map/reduce_scatter | solution.py:613
  1501.6 69.6 %reduce-scatter.50.cloned.1.call-done = bf16[128,1024]{1,0:T(8,128)(2,1)} async-done(((bf16[1024,1024]{1,0:T(8,128)(2,1)}), bf16[128,1024]{1,0:T(8,128)(2,1)}) %reduce-scatter.50.cloned.1.call-update) | async-done | bytes 262160
  1573.1 69.1 %reduce-scatter.34.cloned.1.call-done = bf16[128,1024]{1,0:T(8,128)(2,1)} async-done(((bf16[1024,1024]{1,0:T(8,128)(2,1)}), bf16[128,1024]{1,0:T(8,128)(2,1)}) %reduce-scatter.34.cloned.1.call-update) | async-done | bytes 262160 | tf_op jit(solution)/shard_map/reduce_scatter | solution.py:619
  1644.1 135.6 %reduce-scatter.44.cloned.1.call-done = f32[32,32]{1,0:T(8,128)} async-done(((f32[1024,32]{1,0:T(8,128)}), f32[32,32]{1,0:T(8,128)}) %reduce-scatter.44.cloned.1.call-update) | async-done | bytes 4112 | tf_op jit(solution)/shard_map/reduce_scatter | solution.py:641
  1779.7 134.5 %reduce-scatter.40.cloned.1.call-done = f32[32,64]{1,0:T(8,128)} async-done(((f32[1024,64]{1,0:T(8,128)}), f32[32,64]{1,0:T(8,128)}) %reduce-scatter.40.cloned.1.call-update) | async-done | bytes 8208 | tf_op jit(solution)/shard_map/reduce_scatter | solution.py:639
  1914.2 134.4 %reduce-scatter.42.cloned.1.call-done = f32[32,64]{1,0:T(8,128)} async-done(((f32[1024,64]{1,0:T(8,128)}), f32[32,64]{1,0:T(8,128)}) %reduce-scatter.42.cloned.1.call-update) | async-done | bytes 8208 | tf_op jit(solution)/shard_map/reduce_scatter | solution.py:640
  2048.6 135.2 %reduce-scatter.46.cloned.1.call-done = f32[32,160]{1,0:T(8,128)} async-done(((f32[1024,160]{1,0:T(8,128)}), f32[32,160]{1,0:T(8,128)}) %reduce-scatter.46.cloned.1.call-update) | async-done | bytes 20496 | tf_op jit(solution)/shard_map/reduce_scatter | solution.py:642
  (948 shorter events, 700.0 us)
Async XLA Ops:
  8.1 653.4 %all-reduce.31.cloned.1.call-start = ((), (), s32[]{:S(2)}) async-start(), calls=%async_computation.15 | async-start | bytes 524288 | tf_op jit(solution)/shard_map/psum | solution.py:474
  56.5 414.1 %collective-permute-start = (f32[1,1024]{1,0:T(1,128)S(1)}, f32[1,1024]{1,0:T(1,128)S(1)}, u32[]{:S(2)}, u32[]{:S(2)}) collective-permute-start(f32[1,1024]{1,0:T(1,128)S(1)} %slice_bitcast_fusion.4), channel_id=1, source_target_pairs={{0,4},{4,8},{8,12},{12,16},{16,20},{20,24},{24,28},{1,5},{5,9},{9,... | collective-permute-start | bytes 12296 | tf_op jit(solution)/shard_map/ppermute | solution.py:19
  632.7 47.9 %all-gather.9.cloned.1.call-start = ((), (), s32[]{:S(2)}) async-start(), calls=%async_computation.16 | async-start | bytes 2359296 | tf_op jit(solution)/shard_map/all_gather | solution.py:334
  633.3 98.4 %all-gather.11.cloned.1.call-start = ((), (), s32[]{:S(2)}) async-start(), calls=%async_computation.17 | async-start | bytes 2359296 | tf_op jit(solution)/shard_map/all_gather | solution.py:335
  633.9 143.5 %all-reduce.33.cloned.1.call-start = ((), (), s32[]{:S(2)}) async-start(), calls=%async_computation.19 | async-start | bytes 524288 | tf_op jit(solution)/shard_map/psum | solution.py:510
  737.2 5.5 collective-permute-start.2
  745.9 300.9 %reduce-scatter.36.cloned.1.call-start = ((), (), s32[]{:S(2)}) async-start(), calls=%async_computation.25 | async-start | bytes 36864 | tf_op jit(solution)/shard_map/reduce_scatter | solution.py:625
  946.9 6.1 collective-permute-start.3
  948.4 112.5 %reduce-scatter.38.cloned.1.call-start = ((), (), s32[]{:S(2)}) async-start(), calls=%async_computation.26 | async-start | bytes 36864 | tf_op jit(solution)/shard_map/reduce_scatter | solution.py:628
  950.0 247.9 %reduce-scatter.52.cloned.1.call-start = ((), (), s32[]{:S(2)}) async-start(), calls=%async_computation.33 | async-start | bytes 540672
  959.5 256.8 %reduce-scatter.24.cloned.1.call-start = ((), (), s32[]{:S(2)}) async-start(), calls=%async_computation.18 | async-start | bytes 327680 | tf_op jit(solution)/shard_map/reduce_scatter | solution.py:352
  960.8 278.0 %reduce-scatter.26.cloned.1.call-start = ((), (), s32[]{:S(2)}) async-start(), calls=%async_computation.20 | async-start | bytes 327680 | tf_op jit(solution)/shard_map/reduce_scatter | solution.py:352
  963.1 341.5 %reduce-scatter.48.cloned.1.call-start = ((), (), s32[]{:S(2)}) async-start(), calls=%async_computation.31 | async-start | bytes 589824
  964.6 405.5 %reduce-scatter.28.cloned.1.call-start = ((), (), s32[]{:S(2)}) async-start(), calls=%async_computation.21 | async-start | bytes 589824 | tf_op jit(solution)/shard_map/reduce_scatter | solution.py:607
  965.8 469.4 %reduce-scatter.30.cloned.1.call-start = ((), (), s32[]{:S(2)}) async-start(), calls=%async_computation.22 | async-start | bytes 589824 | tf_op jit(solution)/shard_map/reduce_scatter | solution.py:610
  967.0 533.1 %reduce-scatter.32.cloned.1.call-start = ((), (), s32[]{:S(2)}) async-start(), calls=%async_computation.23 | async-start | bytes 589824 | tf_op jit(solution)/shard_map/reduce_scatter | solution.py:613
  968.3 602.9 %reduce-scatter.50.cloned.1.call-start = ((), (), s32[]{:S(2)}) async-start(), calls=%async_computation.32 | async-start | bytes 2359296
  972.9 669.4 %reduce-scatter.34.cloned.1.call-start = ((), (), s32[]{:S(2)}) async-start(), calls=%async_computation.24 | async-start | bytes 2359296 | tf_op jit(solution)/shard_map/reduce_scatter | solution.py:619
  976.0 803.7 %reduce-scatter.44.cloned.1.call-start = ((), (), s32[]{:S(2)}) async-start(), calls=%async_computation.29 | async-start | bytes 540672 | tf_op jit(solution)/shard_map/reduce_scatter | solution.py:641
  978.0 936.2 %reduce-scatter.40.cloned.1.call-start = ((), (), s32[]{:S(2)}) async-start(), calls=%async_computation.27 | async-start | bytes 540672 | tf_op jit(solution)/shard_map/reduce_scatter | solution.py:639
  980.0 1068.6 %reduce-scatter.42.cloned.1.call-start = ((), (), s32[]{:S(2)}) async-start(), calls=%async_computation.28 | async-start | bytes 540672 | tf_op jit(solution)/shard_map/reduce_scatter | solution.py:640
  982.0 1201.8 %reduce-scatter.46.cloned.1.call-start = ((), (), s32[]{:S(2)}) async-start(), calls=%async_computation.30 | async-start | bytes 1081344 | tf_op jit(solution)/shard_map/reduce_scatter | solution.py:642
  1008.7 37.1 %collective-permute-start.4 = (bf16[24,256]{1,0:T(8,128)(2,1)S(1)}, bf16[24,256]{1,0:T(8,128)(2,1)S(1)}, u32[]{:S(2)}, u32[]{:S(2)}) collective-permute-start(bf16[24,256]{1,0:T(8,128)(2,1)S(1)} %fusion), channel_id=1, source_target_pairs={{0,4},{4,8},{8,12},{12,16},{16,20},{20,24},{24,28},{1,5},{5,9},{9,... | collective-permute-start | bytes 36872
  1010.5 35.3 %collective-permute-start.5 = (bf16[4,256]{1,0:T(4,128)(2,1)S(1)}, bf16[4,256]{1,0:T(4,128)(2,1)S(1)}, u32[]{:S(2)}, u32[]{:S(2)}) collective-permute-start(bf16[4,256]{1,0:T(4,128)(2,1)S(1)} %slice.197), channel_id=1, source_target_pairs={{0,8},{4,12},{8,16},{12,20},{16,24},{20,28},{1,9},{5,13},{9,17},{1... | collective-permute-start | bytes 6152
  (219 other events, 8791.9 us)
Sparse Core Ops, SparseCore 0:
  632.8 28.6 all-reduce.30
  746.0 31.3 all-reduce.32
Sparse Core Ops, SparseCore 1:
  635.3 45.3 all-gather.8
  682.5 49.1 all-gather.10
  948.5 55.2 reduce-scatter.35
  1006.9 54.0 reduce-scatter.37
  1063.2 134.7 reduce-scatter.51
  1200.4 15.9 reduce-scatter.23
  1218.7 20.0 reduce-scatter.25
  1241.9 62.6 reduce-scatter.47
  1308.4 61.6 reduce-scatter.27
  1373.5 61.7 reduce-scatter.29
  1438.4 61.7 reduce-scatter.31
  1503.7 67.5 reduce-scatter.49
  1574.6 67.6 reduce-scatter.33
  1645.1 134.5 reduce-scatter.43
  1782.5 131.6 reduce-scatter.39
  1917.0 131.5 reduce-scatter.41
  2051.5 132.3 reduce-scatter.45
where the time goes:
time: 2200 us; the launch traced here: 2190 us
  waiting for transfers between devices  1240 us (56%)
  blocking collectives  603 us (27%)
  matrix products  182 us (8%)
  other arithmetic  65.7 us (3%)
  local copies, waits for them, and re-layouts  64.7 us (3%)
    unnamed x24, waiting for transfers between devices  271 us
    reduce_scatter x1, waiting for transfers between devices, body(): lax.psum_scatter(grad_mix_down, ('seq', 'head'), scatter_dimension=0, til...  136 us
    reduce_scatter x1, waiting for transfers between devices, body(): lax.psum_scatter(grad_gate_down, ('seq', 'head'), scatter_dimension=0, ti...  135 us
    reduce_scatter x1, waiting for transfers between devices, body(): lax.psum_scatter(grad_decay_down, ('seq', 'head'), scatter_dimension=0, t...  135 us
    reduce_scatter x1, waiting for transfers between devices, body(): lax.psum_scatter(grad_learn_down, ('seq', 'head'), scatter_dimension=0, t...  134 us
    dot_general x113, matrix products, exact_ein(): return jnp.einsum(pattern, former, latter, precision=HIGHEST)  127 us
    reduce_scatter x1, waiting for transfers between devices, body(): lax.psum_scatter(grad_ffn_key.astype(jnp.bfloat16), 'seq', scatter_dimens...  69.1 us
    reduce_scatter x1, waiting for transfers between devices, body(): lax.psum_scatter(grad_recept.astype(jnp.bfloat16), 'seq', scatter_dimensi...  63.8 us
  transfers between devices with their start and end apart: 25, of which 21 were waited for; matrix products, arithmetic and copies ran while one was open for 4% of the time, Pallas kernels for 0%

commit v1 on v0

v1 whole, which is shorter than its diff:
```python
import functools


import jax
import jax.numpy as jnp
from jax import lax
from jax.experimental import pallas as pl
from jax.sharding import PartitionSpec as P

HEAD = 64
CHUNK = 64
INTERPRET = False

NORM_EPS = 1e-05
GROUP_EPS = 0.00064
UNIT_EPS = 1e-06
DECAY_SCALE = 0.606531
BF16 = jnp.bfloat16
F32 = jnp.float32


def shifted_route(axis, distance):
    devices = range(lax.axis_size(axis))
    return [(i, i + distance) for i in devices if i + distance in devices]


def ring_route(axis, distance):
    size = lax.axis_size(axis)
    return [(i, (i + distance) % size) for i in range(size)]


def head_sum(partial_value):
    sent = partial_value.astype(BF16)
    total = partial_value
    for distance in range(1, lax.axis_size("head")):
        total = total + lax.ppermute(sent, "head", ring_route("head", distance)).astype(F32)
    return total


def head_scatter(partial_value, kind=BF16):
    size, place = (lax.axis_size("head"), lax.axis_index("head"))
    width = partial_value.shape[1] // size
    sent = partial_value.astype(kind)
    total = lax.dynamic_slice_in_dim(partial_value, place * width, width, 1)
    for distance in range(1, size):
        block = lax.dynamic_slice_in_dim(sent, (place + distance) % size * width, width, 1)
        total = total + lax.ppermute(block, "head", ring_route("head", distance)).astype(F32)
    return total


def permute_gather(rows, axis):
    size, place = (lax.axis_size(axis), lax.axis_index(axis))
    count = rows.shape[0]
    whole = jnp.zeros((size * count, rows.shape[1]), rows.dtype)
    whole = lax.dynamic_update_slice_in_dim(whole, rows, place * count, 0)
    for distance in range(1, size):
        block = lax.ppermute(rows, axis, ring_route(axis, distance))
        whole = lax.dynamic_update_slice_in_dim(
            whole, block, (place - distance) % size * count, 0
        )
    return whole


def after(value, other):
    never = lax.axis_index("seq") >= lax.axis_size("seq")
    return jnp.where(never, other[(0,) * other.ndim].astype(value.dtype), value)


def stack(parts, axis):
    total = sum(part.shape[axis] for part in parts)
    whole = None
    at = 0
    for part in parts:
        size = part.shape[axis]
        edges = [(0, 0, 0)] * part.ndim
        edges[axis] = (at, total - at - size, 0)
        padded = lax.pad(part, jnp.zeros((), part.dtype), edges)
        whole = padded if whole is None else whole + padded
        at += size
    return whole


def share_out(rows):
    tokens, features = rows.shape
    size = lax.axis_size("seq")
    return rows.reshape(tokens, size, features // size).transpose(1, 0, 2)


def split_three(values):
    high = lax.reduce_precision(values, 8, 7)
    rest = values - high
    middle = lax.reduce_precision(rest, 8, 7)
    return (high.astype(BF16), middle.astype(BF16), (rest - middle).astype(BF16))


def narrow_dot(former, latter):
    return jnp.dot(former.astype(BF16), latter.astype(BF16), preferred_element_type=F32)


def narrow_tn(former, latter):
    return lax.dot_general(
        former.astype(BF16),
        latter.astype(BF16),
        (((0,), (0,)), ((), ())),
        preferred_element_type=F32,
    )


def narrow_nt(former, latter):
    return lax.dot_general(
        former.astype(BF16),
        latter.astype(BF16),
        (((1,), (1,)), ((), ())),
        preferred_element_type=F32,
    )


def standardize(values):
    average = jnp.mean(values, axis=-1, keepdims=True)
    centred = values - average
    spread = jnp.mean(centred * centred, axis=-1, keepdims=True)
    return centred * lax.rsqrt(spread + NORM_EPS)


def layer_norm(values, gain_row, bias_row):
    return standardize(values) * gain_row + bias_row


def shift_mix(normed, previous, weights):
    shifted = jnp.concatenate([previous, normed[:-1]], axis=0)
    difference = shifted - normed
    return tuple((normed + difference * weights[c] for c in range(weights.shape[0])))


def head_sums(values):
    width = values.shape[1]
    return jnp.concatenate(
        [
            jnp.broadcast_to(
                jnp.sum(values[:, at : at + HEAD], axis=1, keepdims=True),
                (values.shape[0], HEAD),
            )
            for at in range(0, width, HEAD)
        ],
        axis=1,
    )


def head_params(refs):
    key_raw, value_raw, decay_shift, learn_shift, mix_shift, first_value = (
        ref[...].astype(F32) for ref in refs[:6]
    )
    table = refs[6]
    decay_gate = jax.nn.sigmoid(table[8:9] + decay_shift)
    rate = jax.nn.sigmoid(table[9:10] + learn_shift)
    mixing = jax.nn.sigmoid(table[10:11] + mix_shift)
    content = value_raw + (first_value - value_raw) * mixing
    scaled_key = key_raw * table[11:12]
    size = lax.rsqrt(head_sums(scaled_key * scaled_key) + UNIT_EPS)
    unit = scaled_key * size
    slope = 1.0 + (rate - 1.0) * table[12:13]
    return dict(
        key_raw=key_raw,
        decay_gate=decay_gate,
        rate=rate,
        mixing=mixing,
        gap=first_value - value_raw,
        size=size,
        unit=unit,
        slope=slope,
        decay_log=-DECAY_SCALE * decay_gate,
        remover=-unit,
        refill=unit * rate,
        key=key_raw * slope,
        content=content,
    )


def head_output(memory, recept, key, content, gates, table):
    centred = memory - head_sums(memory) / HEAD
    spread = lax.rsqrt(head_sums(centred * centred) / HEAD + GROUP_EPS)
    standard = centred * spread
    extra = head_sums(recept * key * table[13:14])
    shown = standard * table[14:15] + table[15:16] + extra * content
    return dict(spread=spread, standard=standard, extra=extra, shown=shown, out=shown * gates)


def token_sum(values):
    return jnp.sum(values, axis=0, keepdims=True)


def split_two(x):
    high = x.astype(BF16)
    return (high, (x - high.astype(F32)).astype(BF16))


NN = (((1,), (0,)), ((), ()))
NT = (((1,), (1,)), ((), ()))
TN = (((0,), (0,)), ((), ()))


def mm(x, y, dims=NN, passes=3):
    def dot(p, q):
        return lax.dot_general(p, q, dims, preferred_element_type=F32)

    if passes == 1:
        return dot(x.astype(BF16), y.astype(BF16))
    xh, xl = split_two(x)
    yh, yl = split_two(y)
    return dot(xh, yh) + (dot(xh, yl) + dot(xl, yh))


def cumulate(mask, x, dims=NN):
    ones = mask.astype(F32).astype(BF16)
    high = x.astype(BF16)
    rest = x - high.astype(F32)
    middle = rest.astype(BF16)
    low = (rest - middle.astype(F32)).astype(BF16)

    def dot(q):
        return lax.dot_general(ones, q, dims, preferred_element_type=F32)

    return dot(high) + (dot(middle) + dot(low))


def masks(tokens, chunk):
    row = lax.broadcasted_iota(jnp.int32, (tokens, tokens), 0)
    col = lax.broadcasted_iota(jnp.int32, (tokens, tokens), 1)
    same = (row // chunk) == (col // chunk)
    strict = same & (col < row)
    inclusive = same & (col <= row)
    return row, col, same, strict, inclusive


def unit_inverse(lower, row, col, chunk):
    eye = jnp.where(row == col, 1.0, 0.0).astype(F32)
    base = min(16, chunk)
    diagonal = jnp.where((row // base) == (col // base), lower, 0.0)
    inverse = eye + diagonal
    power = diagonal
    reach = 2
    while reach < base:
        power = mm(power, power)
        inverse = inverse + mm(inverse, power)
        reach *= 2
    size = base
    while size < chunk:
        size *= 2
        across = jnp.where(
            ((row // size) == (col // size)) & ((row // (size // 2)) != (col // (size // 2))),
            lower,
            0.0,
        )
        inverse = inverse + mm(inverse, mm(across, inverse))
    return inverse


def scaled(decay_log, inclusive, same):
    total = cumulate(inclusive, decay_log)
    ending = cumulate(same, decay_log)
    before = total - decay_log
    return dict(
        ending=ending,
        e_before=jnp.exp(before),
        e_total=jnp.exp(total),
        e_back=jnp.exp(-total),
        e_end=jnp.exp(ending - total),
    )


def head_pieces(ah, rh, bi, ki, v, geometry, chunk):
    row, col, _, strict, inclusive = geometry
    tokens = ah.shape[0]
    pairs = mm(jnp.concatenate([ah, rh], axis=0), jnp.concatenate([bi, ki], axis=0), NT)
    ab = jnp.where(strict, pairs[:tokens, :tokens], 0.0)
    ak = jnp.where(strict, pairs[:tokens, tokens:], 0.0)
    rb = jnp.where(inclusive, pairs[tokens:, :tokens], 0.0)
    rk = jnp.where(inclusive, pairs[tokens:, tokens:], 0.0)
    reads = jnp.concatenate([rb, rk], axis=1)
    inverse = unit_inverse(ab, row, col, chunk)
    u = mm(inverse, mm(ak, v))
    w = mm(inverse, ah)
    reader = rh + mm(rb, w)
    uv = jnp.concatenate([u, v], axis=0)
    base = mm(reads, uv)
    return dict(ak=ak, rb=rb, reads=reads, inverse=inverse, u=u, w=w, uv=uv, reader=reader, base=base)


def head_states(p, be, ke, v, scale, chunk):
    tokens = v.shape[0]
    r64 = lax.broadcasted_iota(jnp.int32, (HEAD, HEAD), 0)
    c64 = lax.broadcasted_iota(jnp.int32, (HEAD, HEAD), 1)
    out = []
    for at in range(0, tokens, chunk):
        s = slice(at, at + chunk)
        diagonal = jnp.where(r64 == c64, jnp.broadcast_to(scale[at : at + 1], (HEAD, HEAD)), 0.0)
        transition = diagonal + mm(p["w"][s], be[s], TN)
        fresh = mm(p["u"][s], be[s], TN) + mm(v[s], ke[s], TN)
        out.append((transition, fresh))
    return out


def members_of(refs):
    p = head_params(refs)
    return p, (
        p["decay_log"], p["remover"], p["refill"], p["key"], p["content"], refs[7][...]
    )


def local_kernel(chunk, *refs):
    tf_ref, rd_ref, ba_ref, sent_ref = refs[RAWS:]
    tokens, width = rd_ref.shape
    geometry = masks(tokens, chunk)
    same, inclusive = (geometry[2], geometry[4])
    decay_log, a, b, k, v, r = members_of(refs[:RAWS])[1]
    e = scaled(decay_log, inclusive, same)
    full = (
        a * e["e_before"],
        r * e["e_total"],
        b * e["e_back"],
        k * e["e_back"],
        b * e["e_end"],
        k * e["e_end"],
        v,
        jnp.exp(e["ending"]),
    )
    for h in range(width // HEAD):
        lanes = slice(h * HEAD, (h + 1) * HEAD)
        ah, rh, bi, ki, be, ke, vh, scale = (x[:, lanes] for x in full)
        p = head_pieces(ah, rh, bi, ki, vh, geometry, chunk)
        rd_ref[:, lanes] = p["reader"]
        ba_ref[:, lanes] = p["base"]
        states = head_states(p, be, ke, vh, scale, chunk)
        total_t = total_f = None
        for c, (transition, fresh) in enumerate(states):
            tf_ref[h, c, :, :HEAD] = transition
            tf_ref[h, c, :, HEAD:] = fresh
            if c == 0:
                total_t, total_f = (transition, fresh)
            else:
                total_f = mm(total_f, transition) + fresh
                total_t = mm(total_t, transition)
        sent_ref[h, :, :HEAD] = total_f.astype(BF16)
        sent_ref[h, :, HEAD:] = total_t.astype(BF16)


def outputs_kernel(count, chunk, *refs):
    got = refs[:count]
    raws = refs[count : count + RAWS]
    tf_ref, rd_ref, ba_ref, gates_ref, out_ref, pre_ref, initial_ref = refs[count + RAWS :]
    tokens, width = rd_ref.shape
    for h in range(width // HEAD):
        lanes = slice(h * HEAD, (h + 1) * HEAD)
        state = jnp.zeros((HEAD, HEAD), F32)
        for g in got:
            state = mm(state, g[h, :, HEAD:].astype(F32)) + g[h, :, :HEAD].astype(F32)
        initial_ref[h] = state
        for c in range(tokens // chunk):
            s = slice(c * chunk, (c + 1) * chunk)
            out_ref[s, lanes] = mm(rd_ref[s, lanes], state, NT) + ba_ref[s, lanes]
            if c + 1 < tokens // chunk:
                state = mm(state, tf_ref[h, c, :, :HEAD]) + tf_ref[h, c, :, HEAD:]
    p = head_params(raws)
    o = head_output(out_ref[...], raws[7][...], p["key"], p["content"], gates_ref[...], raws[6])
    pre_ref[...] = o["out"].astype(BF16)


def local_back_kernel(chunk, *refs):
    raws = refs[:RAWS]
    (
        tf_ref, rd_ref, upper_ref, memory_ref, gates_ref, sent_ref,
        back_ref, g_ref, recept_ref, key_ref, value_ref, gate_ref, table_ref,
    ) = refs[RAWS:]
    tokens, width = rd_ref.shape
    table, recept = (raws[6], raws[7][...])
    p = head_params(raws)
    o = head_output(memory_ref[...], recept, p["key"], p["content"], gates_ref[...], table)
    upper = upper_ref[...]
    gate_ref[...] = (upper * o["shown"]).astype(BF16)
    dshown = upper * gates_ref[...]
    dstandard = dshown * table[14:15]
    g_ref[...] = o["spread"] * (
        dstandard
        - head_sums(dstandard) / HEAD
        - o["standard"] * (head_sums(dstandard * o["standard"]) / HEAD)
    )
    dextra = head_sums(dshown * p["content"])
    value_ref[...] = dshown * o["extra"]
    recept_ref[...] = dextra * p["key"] * table[13:14]
    key_ref[...] = dextra * recept * table[13:14]
    table_ref[0:1] = token_sum(dextra * recept * p["key"])
    table_ref[1:2] = token_sum(dshown * o["standard"])
    table_ref[2:3] = token_sum(dshown)
    for h in range(width // HEAD):
        lanes = slice(h * HEAD, (h + 1) * HEAD)
        grad = None
        for c in reversed(range(tokens // chunk)):
            s = slice(c * chunk, (c + 1) * chunk)
            own = mm(g_ref[s, lanes], rd_ref[s, lanes], TN)
            grad = own if grad is None else mm(grad, tf_ref[h, c, :, :HEAD], NT) + own
        back_ref[h, :, :HEAD] = grad.astype(BF16)
        back_ref[h, :, HEAD:] = sent_ref[h, :, HEAD:]


def back_kernel(count, chunk, *refs):
    got = refs[:count]
    raws = refs[count : count + RAWS]
    (
        initial_ref, tf_ref, rd_ref, g_ref, recept_ref, key_ref, value_ref,
        dr_ref, dk_ref, dv_ref, ddecay_ref, dlearn_ref, dmix_ref, first_ref, table_ref,
    ) = refs[count + RAWS :]
    tokens, width = rd_ref.shape
    chunks = tokens // chunk
    geometry = masks(tokens, chunk)
    _, _, same, strict, inclusive = geometry
    r64 = lax.broadcasted_iota(jnp.int32, (HEAD, HEAD), 0)
    c64 = lax.broadcasted_iota(jnp.int32, (HEAD, HEAD), 1)
    raw, (decay_log, a, b, k, v, r) = members_of(raws)
    e = scaled(decay_log, inclusive, same)
    ah_f, rh_f, bi_f, ki_f, be_f, ke_f = (
        a * e["e_before"],
        r * e["e_total"],
        b * e["e_back"],
        k * e["e_back"],
        b * e["e_end"],
        k * e["e_end"],
    )
    scale_f = jnp.exp(e["ending"])
    dah_l, drh_l, dbi_l, dki_l, dbe_l, dke_l, dv_l, dend_l = ([] for _ in range(8))
    for h in range(width // HEAD):
        lanes = slice(h * HEAD, (h + 1) * HEAD)
        ah, rh, bi, ki, be, ke, vh, _ = (
            x[:, lanes] for x in (ah_f, rh_f, bi_f, ki_f, be_f, ke_f, v, scale_f)
        )
        g = g_ref[:, lanes]
        p = head_pieces(ah, rh, bi, ki, vh, geometry, chunk)
        u, w = (p["u"], p["w"])
        starts = [initial_ref[h]]
        for c in range(chunks - 1):
            starts.append(mm(starts[c], tf_ref[h, c, :, :HEAD]) + tf_ref[h, c, :, HEAD:])
        grad = jnp.zeros((HEAD, HEAD), F32)
        for m in got:
            grad = mm(grad, m[h, :, HEAD:].astype(F32), NT) + m[h, :, :HEAD].astype(F32)
        nexts = [None] * chunks
        for c in reversed(range(chunks)):
            nexts[c] = grad
            if c:
                s = slice(c * chunk, (c + 1) * chunk)
                grad = mm(grad, tf_ref[h, c, :, :HEAD], NT) + mm(g[s], rd_ref[s, lanes], TN)
        dw, du, dv, dbe, dke, dreader, dend = ([] for _ in range(7))
        for c in range(chunks):
            s = slice(c * chunk, (c + 1) * chunk)
            dt = mm(starts[c], nexts[c], TN)
            df = nexts[c]
            dreader.append(mm(g[s], starts[c]))
            dw.append(mm(be[s], dt, NT))
            du.append(mm(be[s], df, NT))
            dv.append(mm(ke[s], df, NT))
            dbe.append(mm(w[s], dt) + mm(u[s], df))
            dke.append(mm(vh[s], df))
            line = jnp.sum(jnp.where(r64 == c64, dt, 0.0), axis=0, keepdims=True)
            dend.append(jnp.broadcast_to(line, (chunk, HEAD)))
        dw, du, dv, dbe, dke, dreader, dend = (
            jnp.concatenate(x, axis=0) for x in (dw, du, dv, dbe, dke, dreader, dend)
        )
        dreads = mm(g, p["uv"], NT)
        drb = jnp.where(inclusive, mm(dreader, w, NT) + dreads[:, :tokens], 0.0)
        drk = jnp.where(inclusive, dreads[:, tokens:], 0.0)
        duv = mm(p["reads"], g, TN)
        dw = dw + mm(p["rb"], dreader, TN)
        du = du + duv[:tokens]
        dz = mm(p["inverse"], du, TN)
        q = mm(p["inverse"], dw, TN)
        dsolve = mm(dz, p["uv"], NT)
        dab = jnp.where(strict, mm(q, w, NT) + dsolve[:, :tokens], 0.0)
        dak = jnp.where(strict, dsolve[:, tokens:], 0.0)
        dv = dv + duv[tokens:] + mm(p["ak"], dz, TN)
        dpairs = jnp.concatenate(
            [jnp.concatenate([dab, dak], axis=1), jnp.concatenate([drb, drk], axis=1)], axis=0
        )
        dleft = mm(dpairs, jnp.concatenate([bi, ki], axis=0))
        dright = mm(dpairs, jnp.concatenate([ah, rh], axis=0), TN)
        dah_l.append(q + dleft[:tokens])
        drh_l.append(dreader + dleft[tokens:])
        dbi_l.append(dright[:tokens])
        dki_l.append(dright[tokens:])
        dbe_l.append(dbe)
        dke_l.append(dke)
        dv_l.append(dv)
        dend_l.append(dend)
    dah, drh, dbi, dki, dbe, dke, dv, dend = (
        jnp.concatenate(x, axis=1)
        for x in (dah_l, drh_l, dbi_l, dki_l, dbe_l, dke_l, dv_l, dend_l)
    )
    da = dah * e["e_before"]
    dr = drh * e["e_total"] + recept_ref[...]
    db = dbi * e["e_back"] + dbe * e["e_end"]
    dk = dki * e["e_back"] + dke * e["e_end"] + key_ref[...]
    dv = dv + value_ref[...]
    dbefore = dah * ah_f
    at_end = dbe * be_f + dke * ke_f
    dtotal = dbefore + drh * rh_f - dbi * bi_f - dki * ki_f - at_end
    dl = cumulate(inclusive, dtotal, TN) - dbefore + cumulate(same, at_end) + dend * scale_f
    table = raws[6]
    key_raw, rate, mixing, unit = (raw["key_raw"], raw["rate"], raw["mixing"], raw["unit"])
    ddecay = dl * (-DECAY_SCALE) * raw["decay_gate"] * (1.0 - raw["decay_gate"])
    dslope = dk * key_raw
    dlearn = (db * unit + dslope * table[12:13]) * rate * (1.0 - rate)
    dmix = dv * raw["gap"] * mixing * (1.0 - mixing)
    dunit = db * rate - da
    dscaled = raw["size"] * (dunit - unit * head_sums(dunit * unit))
    first_ref[...] = dv * mixing
    dr_ref[...] = dr.astype(BF16)
    dk_ref[...] = (dscaled * table[11:12] + dk * raw["slope"]).astype(BF16)
    dv_ref[...] = (dv * (1.0 - mixing)).astype(BF16)
    ddecay_ref[...] = ddecay.astype(BF16)
    dlearn_ref[...] = dlearn.astype(BF16)
    dmix_ref[...] = dmix.astype(BF16)
    table_ref[0:1] = token_sum(ddecay)
    table_ref[1:2] = token_sum(dlearn)
    table_ref[2:3] = token_sum(dmix)
    table_ref[3:4] = token_sum(dscaled * key_raw)
    table_ref[4:5] = token_sum(dslope * (rate - 1.0))


RAWS = 8


def chunk_of(tokens):
    return min(tokens, CHUNK)


def pairs_of(channels):
    return 2 if channels % (2 * HEAD) == 0 else channels // HEAD


def wkv_call(kernel, channels, inputs, outs):
    group = pairs_of(channels)
    width = group * HEAD

    def spec(shape):
        if len(shape) == 2:
            return pl.BlockSpec((shape[0], width), lambda i: (0, i))
        rest = tuple(shape[1:])
        return pl.BlockSpec((group,) + rest, lambda i: (i,) + (0,) * len(rest))

    return pl.pallas_call(
        kernel,
        grid=(channels // width,),
        in_specs=[spec(x.shape) for x in inputs],
        out_specs=[spec(s) for s, _ in outs],
        out_shape=[jax.ShapeDtypeStruct(s, d) for s, d in outs],
        interpret=INTERPRET,
    )(*inputs)


def wkv_local(raws):
    tokens, channels = raws[0].shape
    heads, chunk = (channels // HEAD, chunk_of(tokens))
    return wkv_call(
        functools.partial(local_kernel, chunk),
        channels,
        raws,
        [
            ((heads, tokens // chunk, HEAD, 2 * HEAD), F32),
            ((tokens, channels), F32),
            ((tokens, channels), F32),
            ((heads, HEAD, 2 * HEAD), BF16),
        ],
    )


def wkv_outputs(got, raws, tf, reader, base, gates):
    tokens, channels = reader.shape
    heads, chunk = (channels // HEAD, chunk_of(tokens))
    return wkv_call(
        functools.partial(outputs_kernel, len(got), chunk),
        channels,
        [*got, *raws, tf, reader, base, gates],
        [
            ((tokens, channels), F32),
            ((tokens, channels), BF16),
            ((heads, HEAD, HEAD), F32),
        ],
    )


def wkv_local_back(raws, tf, reader, upper, memory, gates, sent):
    tokens, channels = reader.shape
    return wkv_call(
        functools.partial(local_back_kernel, chunk_of(tokens)),
        channels,
        [*raws, tf, reader, upper, memory, gates, sent],
        [(sent.shape, BF16)]
        + [((tokens, channels), F32)] * 4
        + [((tokens, channels), BF16), ((3, channels), F32)],
    )


def wkv_back(got, raws, initial, tf, reader, grad, parts):
    tokens, channels = reader.shape
    return wkv_call(
        functools.partial(back_kernel, len(got), chunk_of(tokens)),
        channels,
        [*got, *raws, initial, tf, reader, grad, *parts],
        [
            *[((tokens, channels), BF16)] * 6,
            ((tokens, channels), F32),
            ((5, channels), F32),
        ],
    )


def state_exchange(values, distance_sign):
    size = lax.axis_size("seq")
    return [
        lax.ppermute(values, "seq", shifted_route("seq", distance_sign * distance))
        for distance in range(size - 1, 0, -1)
    ]


def body(
    layer_input,
    first_layer_value,
    cotangent,
    receptance_weight,
    key_weight,
    value_weight,
    output_weight,
    channel_key_weight,
    channel_value_weight,
    decay_second_factor,
    learn_second_factor,
    residual_second_factor,
    gate_second_factor,
    decay_first_factor,
    learn_first_factor,
    residual_first_factor,
    gate_first_factor,
    vectors,
):
    sequences, tokens, features = layer_input.shape
    assert sequences == 1
    channels = first_layer_value.shape[2]
    hidden_units = channel_key_weight.shape[1]
    seq_size, seq_place = (lax.axis_size("seq"), lax.axis_index("seq"))
    head_size, head_place = (lax.axis_size("head"), lax.axis_index("head"))
    offset = head_place * channels
    share = features // seq_size
    small_share = features // (seq_size * head_size)

    x_bf = layer_input.reshape(tokens, features)
    x_rows = x_bf.astype(F32)
    cot_bf = cotangent.reshape(tokens, features)
    previous_x = lax.ppermute(x_bf[-1:], "seq", shifted_route("seq", 1)).astype(F32)
    has_previous = (seq_place > 0).astype(F32)

    firsts = (decay_first_factor, learn_first_factor, residual_first_factor, gate_first_factor)
    ranks = [member.shape[1] for member in firsts]
    columns = vectors.shape[1]
    small = jnp.concatenate(firsts + split_three(vectors), axis=1)
    seconds = (
        decay_second_factor,
        learn_second_factor,
        residual_second_factor,
        gate_second_factor,
    )
    second_rows = [member.shape[0] for member in seconds]
    payload = stack(
        [receptance_weight, key_weight, value_weight, output_weight.T, *seconds], 0
    )
    gathered = lax.all_gather(payload, "seq", axis=0, tiled=False)
    cuts = []
    at = 0
    for rows in [share] * 4 + second_rows:
        cuts.append(gathered[:, at : at + rows].reshape(seq_size * rows, channels))
        at += rows
    recept_cols, key_cols, value_cols, out_cols, decay_up, learn_up, mix_up, gate_up = cuts

    shared = lax.all_to_all(
        jnp.concatenate([share_out(standardize(x_rows).astype(BF16)), share_out(cot_bf)], axis=2),
        "seq",
        split_axis=0,
        concat_axis=0,
        tiled=True,
    )
    standard_all = shared[..., :share].reshape(seq_size * tokens, share)
    cot_all = shared[..., share:].reshape(seq_size * tokens, share)

    small_all = permute_gather(after(small, payload), "seq")
    small_all = permute_gather(small_all, "head")
    small_all = (
        small_all.reshape(head_size, seq_size, small_share, -1)
        .transpose(1, 0, 2, 3)
        .reshape(features, -1)
    )
    downs = []
    at = 0
    for rank in ranks:
        downs.append(small_all[:, at : at + rank])
        at += rank
    decay_down, learn_down, mix_down, gate_down = downs
    pieces = small_all[:, at : at + 3 * columns].astype(F32)
    vec = (
        pieces[:, :columns] + pieces[:, columns : 2 * columns] + pieces[:, 2 * columns :]
    ).T
    local_vec = lax.dynamic_slice_in_dim(vec, offset, channels, 1)

    ffn_payload = after(
        jnp.concatenate([channel_key_weight, channel_value_weight.T], axis=1), shared
    )
    ffn_gathered = lax.all_gather(ffn_payload, "seq", axis=0, tiled=True)
    ffn_key_cols = ffn_gathered[:, :hidden_units]
    ffn_value_cols = ffn_gathered[:, hidden_units:]

    def first_norm(values, table):
        return layer_norm(values, table[0], table[1])

    def second_norm(values, table):
        return layer_norm(values, table[16], table[17])

    def time_inputs(normed, previous, table):
        return shift_mix(normed, previous, table[2:8])

    def ffn_inputs(normed, previous, table):
        return shift_mix(normed, previous, table[18:19])[0]

    normed_a = first_norm(x_rows, vec)
    prev_a = first_norm(previous_x, vec) * has_previous
    mixes = time_inputs(normed_a, prev_a, vec)
    mixed_recept, mixed_decay, mixed_key, mixed_value, mixed_learn, mixed_gate = mixes
    recept = narrow_dot(mixed_recept, recept_cols)
    key_raw = narrow_dot(mixed_key, key_cols)
    value_raw = narrow_dot(mixed_value, value_cols)
    decay_low = narrow_dot(mixed_decay, decay_down)
    learn_low = narrow_dot(mixed_learn, learn_down)
    mix_low = narrow_dot(mixed_value, mix_down)
    gate_low = narrow_dot(mixed_gate, gate_down)
    decay_tanh = jnp.tanh(decay_low)
    gate_sigm = jax.nn.sigmoid(gate_low)
    decay_shift = narrow_dot(decay_tanh, decay_up)
    learn_shift = narrow_dot(learn_low, learn_up)
    mix_shift = narrow_dot(mix_low, mix_up)
    gates = narrow_dot(gate_sigm, gate_up)
    first_value = first_layer_value.reshape(tokens, channels)
    raws = (
        key_raw, value_raw, decay_shift, learn_shift, mix_shift, first_value, local_vec, recept
    )
    states, reader, base, sent = wkv_local(raws)
    memory_out, pre_out, initial = wkv_outputs(
        state_exchange(sent, 1), raws, states, reader, base, gates
    )
    middle = x_rows + head_sum(narrow_nt(pre_out, out_cols))
    normed_b, norm_b_back = jax.vjp(second_norm, middle, vec)
    prev_b = lax.ppermute(normed_b[-1:], "seq", shifted_route("seq", 1))
    mixed_ffn, ffn_back = jax.vjp(ffn_inputs, normed_b, prev_b, vec)
    middle_share = lax.dynamic_slice_in_dim(middle, offset, channels, 1)
    hidden_pre = narrow_dot(mixed_ffn, ffn_key_cols)
    active = jnp.maximum(hidden_pre, 0.0)
    hidden = active * active
    result = middle_share + head_scatter(narrow_nt(hidden, ffn_value_cols))
    pre_grad = narrow_dot(cot_bf, ffn_value_cols) * 2.0 * active
    ffn_rows = lax.all_gather(
        jnp.concatenate([member.astype(BF16) for member in (hidden, pre_grad, pre_out)], axis=1),
        "seq",
        axis=0,
        tiled=True,
    )
    ffn_back_part = narrow_nt(pre_grad, ffn_key_cols)
    normed_b_grad, prev_b_grad, vec_ffn_mix = ffn_back(ffn_back_part)
    returned_b = lax.ppermute(prev_b_grad, "seq", shifted_route("seq", -1))
    normed_b_grad = jnp.concatenate([normed_b_grad[:-1], normed_b_grad[-1:] + returned_b], axis=0)
    middle_part, vec_ffn_norm = norm_b_back(normed_b_grad)
    middle_grad = cot_bf.astype(F32) + head_sum(middle_part)
    middle_grad_share = lax.dynamic_slice_in_dim(middle_grad, offset, channels, 1)
    pre_out_grad = narrow_dot(middle_grad, out_cols)
    sent_back, memory_grad, recept_part, key_part, value_part, gate_grad, table_out = (
        wkv_local_back(raws, states, reader, pre_out_grad, memory_out, gates, sent)
    )
    grad_gate_up = narrow_tn(gate_sigm, gate_grad)
    gate_low_grad = narrow_nt(gate_grad, gate_up) * gate_sigm * (1.0 - gate_sigm)
    *row_grads, first_grad, table_param = wkv_back(
        state_exchange(sent_back, -1),
        raws,
        initial,
        states,
        reader,
        memory_grad,
        (recept_part, key_part, value_part),
    )
    decay_shift_grad, learn_shift_grad, mix_shift_grad = row_grads[3:]
    decay_low_grad = narrow_nt(decay_shift_grad, decay_up) * (1.0 - decay_tanh * decay_tanh)
    learn_low_grad = narrow_nt(learn_shift_grad, learn_up)
    mix_low_grad = narrow_nt(mix_shift_grad, mix_up)
    low_grad = head_sum(
        jnp.concatenate([decay_low_grad, learn_low_grad, mix_low_grad, gate_low_grad], axis=1)
    )
    final = jnp.concatenate(
        [*row_grads[:3], low_grad.astype(BF16)], axis=1
    )
    sent_final = after(final, ffn_rows)
    final = lax.all_gather(sent_final, "seq", axis=0, tiled=True)
    second_grads = (
        narrow_tn(decay_tanh, after(decay_shift_grad, sent_final)),
        narrow_tn(learn_low, after(learn_shift_grad, sent_final)),
        narrow_tn(mix_low, after(mix_shift_grad, sent_final)),
        grad_gate_up,
    )
    second_parts = []
    for member, rows in zip(second_grads, second_rows):
        member = member.astype(BF16).reshape(seq_size, rows, channels)
        second_parts += [member[..., at : at + share] for at in range(0, channels, share)]
    recept_sent, key_sent, value_sent = (
        sent_final[:, c * channels : (c + 1) * channels] for c in range(3)
    )
    mixes_grad = (
        narrow_nt(recept_sent, recept_cols),
        narrow_nt(after(decay_low_grad, sent_final), decay_down),
        narrow_nt(key_sent, key_cols),
        narrow_nt(value_sent, value_cols) + narrow_nt(after(mix_low_grad, sent_final), mix_down),
        narrow_nt(after(learn_low_grad, sent_final), learn_down),
        narrow_nt(after(gate_low_grad, sent_final), gate_down),
    )
    _, mix_back = jax.vjp(time_inputs, normed_a, prev_a, vec)
    normed_a_grad, prev_a_grad, vec_attn_mix = mix_back(mixes_grad)
    returned_a = lax.ppermute(prev_a_grad, "seq", shifted_route("seq", -1))
    normed_a_grad = jnp.concatenate([normed_a_grad[:-1], normed_a_grad[-1:] + returned_a], axis=0)
    _, norm_a_back = jax.vjp(first_norm, x_rows, vec)
    input_part, vec_attn_norm = norm_a_back(normed_a_grad)
    input_grad = middle_grad_share + head_scatter(input_part)

    table_local = jnp.concatenate([table_param, table_out], axis=0)
    vec_grad = lax.dynamic_update_slice(
        vec_ffn_mix + vec_ffn_norm + vec_attn_mix + vec_attn_norm, table_local, (8, offset)
    )
    vec_split = vec_grad.reshape(columns, seq_size, share).transpose(1, 0, 2)
    vec_high, vec_low, _ = split_three(vec_split)
    last = lax.all_to_all(
        stack(
            [share_out(mixed_ffn.astype(BF16)), share_out(middle_grad.astype(BF16))]
            + [*second_parts, vec_high, vec_low],
            1,
        ),
        "seq",
        split_axis=0,
        concat_axis=0,
        tiled=True,
    )
    mixed_all = last[:, :tokens].reshape(seq_size * tokens, share)
    middle_grad_all = last[:, tokens : 2 * tokens].reshape(seq_size * tokens, share)
    sums = jnp.sum(last[:, 2 * tokens :].astype(F32), axis=0)
    second_sum = sums[: -2 * columns]
    vec_seq = sums[-2 * columns : -columns] + sums[-columns:]
    vec_mine = head_scatter(vec_seq, F32).T

    share_vec = lax.dynamic_slice_in_dim(vec, seq_place * share, share, 1)
    normed_all = standard_all.astype(F32) * share_vec[0] + share_vec[1]
    zero_row = jnp.zeros((1, share), F32)
    recept_all, decay_all, key_all, value_all, learn_all, gate_all = shift_mix(
        normed_all, zero_row, share_vec[2:8]
    )
    grad_recept = narrow_tn(recept_all, final[:, :channels])
    grad_key = narrow_tn(key_all, final[:, channels : 2 * channels])
    grad_value = narrow_tn(value_all, final[:, 2 * channels : 3 * channels])
    first_outs = []
    at = 3 * channels
    for member, rank in zip((decay_all, learn_all, value_all, gate_all), ranks):
        mine = lax.dynamic_slice_in_dim(member, head_place * small_share, small_share, 1)
        first_outs.append(narrow_tn(mine, final[:, at : at + rank]))
        at += rank

    hidden_all = ffn_rows[:, :hidden_units]
    pre_grad_all = ffn_rows[:, hidden_units : 2 * hidden_units]
    pre_out_all = ffn_rows[:, 2 * hidden_units :]
    second_outs = []
    at = 0
    for rows in second_rows:
        parts = []
        for _ in range(0, channels, share):
            parts.append(second_sum[at : at + rows])
            at += rows
        second_outs.append(jnp.concatenate(parts, axis=1))
    return (
        result[None],
        input_grad[None],
        first_grad[None],
        grad_recept,
        grad_key,
        grad_value,
        narrow_tn(pre_out_all, middle_grad_all),
        narrow_tn(mixed_all, pre_grad_all),
        narrow_tn(hidden_all, cot_all),
        *second_outs,
        *first_outs,
        vec_mine,
    )


def solution(mesh):
    placed = (
        P(None, "seq", None),
        P(None, "seq", "head"),
        P(None, "seq", None),
        P("seq", "head"),
        P("seq", "head"),
        P("seq", "head"),
        P("head", "seq"),
        P("seq", "head"),
        P("head", "seq"),
        P("seq", "head"),
        P("seq", "head"),
        P("seq", "head"),
        P("seq", "head"),
        P(("seq", "head"), None),
        P(("seq", "head"), None),
        P(("seq", "head"), None),
        P(("seq", "head"), None),
        P(("seq", "head"), None),
    )
    return jax.shard_map(
        body,
        mesh=mesh,
        in_specs=placed,
        out_specs=(
            P(None, "seq", "head"),
            P(None, "seq", "head"),
            P(None, "seq", "head"),
            P("seq", "head"),
            P("seq", "head"),
            P("seq", "head"),
            P("head", "seq"),
            P("seq", "head"),
            P("head", "seq"),
            P("seq", "head"),
            P("seq", "head"),
            P("seq", "head"),
            P("seq", "head"),
            P(("seq", "head"), None),
            P(("seq", "head"), None),
            P(("seq", "head"), None),
            P(("seq", "head"), None),
            P(("seq", "head"), None),
        ),
        check_vma=False,
    )
```

time: 2200 us -> 373 us (0.17)
  waiting for transfers between devices: 1240 us -> 102 us
  blocking collectives: 603 us -> 0 us
  matrix products: 182 us -> 58.1 us
  starting transfers between devices: 11.6 us -> 87 us
  Pallas kernels: 0 us -> 45.6 us
  other arithmetic: 65.7 us -> 27.4 us
  local copies, waits for them, and re-layouts: 64.7 us -> 31 us
    reduce_scatter x12 -> x0, waiting for transfers between devices: 850 us -> none  [the longest x1 136 us: body(): lax.psum_scatter(grad_mix_down, ('seq', 'head'), scatter_dimension=0, til...]
    all_gather x16 -> x0, blocking collectives: 547 us -> none  [the longest x2 62.7 us: carried_in(): lax.all_gather(part.astype(kind), axis)]
    unnamed x24 -> x4, waiting for transfers between devices: 271 us -> 0.07 us
    dot_general x171 -> x42, matrix products: 182 us -> 58.1 us  [the longest x14 24.9 us: narrow_tn(): lax.dot_general(former.astype(BF16), latter.astype(BF16), (((0,), (0,)),...]
    ppermute x4 -> x46, starting transfers between devices: 7.68 us -> 67.6 us  [the longest x10 24.3 us: permute_gather(): block = lax.ppermute(rows, axis, ring_route(axis, distance))]
    unnamed x2 -> x0, blocking collectives: 55.6 us -> none
    psum x2 -> x0, waiting for transfers between devices: 54.2 us -> none  [the longest x1 27.6 us: body(): lax.psum(partial_value.astype(jnp.bfloat16), 'head').astype(jnp.float32)]
    ppermute x4 -> x46, waiting for transfers between devices: 7.2 us -> 58.8 us  [the longest x9 23.6 us: head_sum(): lax.ppermute(sent, 'head', ring_route('head', distance)).astype(F32)]
  transfers between devices with their start and end apart: 25 -> 52, of which waited for: 21 -> 24; matrix products, arithmetic and copies ran while one was open for 4% -> 21% of each run, Pallas kernels for 0% -> 12%
where the time goes in v1:
time: 373 us; the launch traced here: 369 us
  waiting for transfers between devices  102 us (27%)
  starting transfers between devices  87 us (23%)
  matrix products  58.1 us (16%)
  Pallas kernels  45.6 us (12%)
  local copies, waits for them, and re-layouts  31 us (8%)
  other arithmetic  27.4 us (7%)
  between operations  17.5 us (5%)
    pallas_call x4, Pallas kernels, wkv_call(): pl.pallas_call(kernel, grid=(channels // width,), in_specs=[spec(x.shape)...  45.6 us
    all_to_all x1, waiting for transfers between devices, body(): lax.all_to_all(stack([share_out(mixed_ffn.astype(BF16)), share_out(middle...  27.3 us
    dot_general x14, matrix products, narrow_tn(): lax.dot_general(former.astype(BF16), latter.astype(BF16), (((0,), (0,)),...  24.9 us
    ppermute x10, starting transfers between devices, permute_gather(): block = lax.ppermute(rows, axis, ring_route(axis, distance))  24.3 us
    ppermute x14, starting transfers between devices, state_exchange(): lax.ppermute(values, 'seq', shifted_route('seq', distance_sign * distance))  23.9 us
    ppermute x9, waiting for transfers between devices, head_sum(): lax.ppermute(sent, 'head', ring_route('head', distance)).astype(F32)  23.6 us
    dot_general x14, matrix products, narrow_nt(): lax.dot_general(former.astype(BF16), latter.astype(BF16), (((1,), (1,)),...  17.4 us
    dot_general x14, matrix products, narrow_dot(): jnp.dot(former.astype(BF16), latter.astype(BF16), preferred_element_type=...  15.9 us
  transfers between devices with their start and end apart: 52, of which 24 were waited for; matrix products, arithmetic and copies ran while one was open for 21% of the time, Pallas kernels for 12%

profile of v1, /device:TPU:0, one launch (start us, length us, event | category | flops | bytes accessed | tf_op | source)
XLA Modules:
  0.0 369.1 jit_solution(11717963595827342348)
XLA Ops:
  13.6 7.3 %all-to-all-start = ((bf16[8,128,256]{1,2,0:T(8,128)(2,1)}), bf16[8,128,256]{1,2,0:T(8,128)(2,1)S(1)}, u32[]{:S(2)}, u32[]{:S(2)}) async-start(bf16[8,128,256]{1,2,0:T(8,128)(2,1)} %pad_maximum_fusion.1), calls=%async_computation | async-start | bytes 1048576 | tf_op jit(solution)/shard_map/all_to_all | solution.py:680
  34.4 5.3 %collective-permute-start.4 = (bf16[32,377]{1,0:T(8,128)(2,1)S(1)}, bf16[32,377]{1,0:T(8,128)(2,1)S(1)}, u32[]{:S(2)}, u32[]{:S(2)}) collective-permute-start(bf16[32,377]{1,0:T(8,128)(2,1)S(1)} %get-tuple-element.87), channel_id=1, source_target_pairs={{0,20},{4,24},{8,28},{12,0},{16,4},{20,8},{24,12},{28,16},{1,21},{... | collective-permute-start | bytes 72392 | tf_op jit(solution)/shard_map/ppermute | solution.py:57
  40.9 3.9 %collective-permute-done = bf16[32,377]{1,0:T(8,128)(2,1)S(1)} collective-permute-done((bf16[32,377]{1,0:T(8,128)(2,1)S(1)}, bf16[32,377]{1,0:T(8,128)(2,1)S(1)}, u32[]{:S(2)}, u32[]{:S(2)}) %collective-permute-start) | collective-permute-done | bytes 24160 | tf_op jit(solution)/shard_map/ppermute | solution.py:57
  44.8 6.7 %collective-permute-start.5 = (bf16[32,377]{1,0:T(8,128)(2,1)S(1)}, bf16[32,377]{1,0:T(8,128)(2,1)S(1)}, u32[]{:S(2)}, u32[]{:S(2)}) collective-permute-start(bf16[32,377]{1,0:T(8,128)(2,1)S(1)} %get-tuple-element.87), channel_id=1, source_target_pairs={{0,24},{4,28},{8,0},{12,4},{16,8},{20,12},{24,16},{28,20},{1,25},{... | collective-permute-start | bytes 72392 | tf_op jit(solution)/shard_map/ppermute | solution.py:57
  61.7 3.5 collective-permute-done.8
  70.7 3.6 all-gather.12.cloned.1.call-done
  84.2 11.5 %shard_map.313 = (f32[4,2,64,128]{3,2,1,0:T(8,128)}, f32[128,256]{1,0:T(8,128)}, f32[128,256]{1,0:T(8,128)}, bf16[4,64,128]{2,1,0:T(8,128)(2,1)}) custom-call(f32[128,256]{1,0:T(8,128)} %fusion.49.refs_0_.refs_7_, f32[128,256]{1,0:T(8,128)} %fusion.52.refs_1_.refs_8_, f32[128,256]{1,0:T(8,128)} %fusion.118.refs_2_.refs_9_, ...), custom_call_target="tpu_custom_call" | custom-call | tf_op jit(solution)/shard_map/pallas_call | solution.py:547
  95.7 4.2 %collective-permute-start.11 = (bf16[4,64,128]{2,1,0:T(8,128)(2,1)}, bf16[4,64,128]{2,1,0:T(8,128)(2,1)S(1)}, u32[]{:S(2)}, u32[]{:S(2)}) collective-permute-start(bf16[4,64,128]{2,1,0:T(8,128)(2,1)} %get-tuple-element.40.refs_13_), channel_id=1, source_target_pairs={{0,28},{1,29},{2,30},{3,31}} | collective-permute-start | bytes 196616 | tf_op jit(solution)/shard_map/ppermute | solution.py:617
  115.0 8.0 %shard_map.314 = (f32[128,256]{1,0:T(8,128)}, bf16[128,256]{1,0:T(8,128)(2,1)}, f32[4,64,64]{2,1,0:T(8,128)}) custom-call(bf16[4,64,128]{2,1,0:T(8,128)(2,1)} %copy-done.52, bf16[4,64,128]{2,1,0:T(8,128)(2,1)} %copy-done.54, bf16[4,64,128]{2,1,0:T(8,128)(2,1)} %copy-done.56, bf16[4,64,128]{2,1,0:T(8,128)(2,1)} %copy-done.57, bf16[4,64,128]{2,1,0:T(8,128)(2,1)} %copy-done.58, ...), custom_call_target="tpu_custom_call" | custom-call | tf_op jit(solution)/shard_map/pallas_call | solution.py:547
  125.9 4.0 %collective-permute-done.20 = bf16[128,1024]{1,0:T(8,128)(2,1)S(1)} collective-permute-done((bf16[128,1024]{1,0:T(8,128)(2,1)S(1)}, bf16[128,1024]{1,0:T(8,128)(2,1)S(1)}, u32[]{:S(2)}, u32[]{:S(2)}) %collective-permute-start.20) | collective-permute-done | bytes 262176 | tf_op jit(solution)/shard_map/ppermute | solution.py:36
  130.0 8.4 %collective-permute-done.19 = bf16[128,1024]{1,0:T(8,128)(2,1)S(1)} collective-permute-done((bf16[128,1024]{1,0:T(8,128)(2,1)S(1)}, bf16[128,1024]{1,0:T(8,128)(2,1)S(1)}, u32[]{:S(2)}, u32[]{:S(2)}) %collective-permute-start.19) | collective-permute-done | bytes 262176 | tf_op jit(solution)/shard_map/ppermute | solution.py:36
  139.1 4.4 %collective-permute-start.21 = (f32[1,1024]{1,0:T(1,128)S(1)}, f32[1,1024]{1,0:T(1,128)S(1)}, u32[]{:S(2)}, u32[]{:S(2)}) collective-permute-start(f32[1,1024]{1,0:T(1,128)S(1)} %slice.416), channel_id=1, source_target_pairs={{0,4},{4,8},{8,12},{12,16},{16,20},{20,24},{24,28},{1,5},{5,9},{9,... | collective-permute-start | bytes 12296 | tf_op jit(solution)/shard_map/ppermute | solution.py:755
  145.0 12.8 %all-gather.6.cloned.1.call-done = bf16[1024,2048]{0,1:T(8,128)(2,1)} async-done(((bf16[128,2048]{0,1:T(8,128)(2,1)}), bf16[1024,2048]{0,1:T(8,128)(2,1)}) %all-gather.6.cloned.1.call-update) | async-done | bytes 4194320 | tf_op jit(solution)/shard_map/all_gather | solution.py:712
  176.1 3.4 collective-permute-done.25
  184.7 4.3 %collective-permute-done.28 = bf16[128,1024]{1,0:T(8,128)(2,1)S(1)} collective-permute-done((bf16[128,1024]{1,0:T(8,128)(2,1)S(1)}, bf16[128,1024]{1,0:T(8,128)(2,1)S(1)}, u32[]{:S(2)}, u32[]{:S(2)}) %collective-permute-start.28) | collective-permute-done | bytes 262176 | tf_op jit(solution)/shard_map/ppermute | solution.py:36
  188.9 6.7 %collective-permute-done.27 = bf16[128,1024]{1,0:T(8,128)(2,1)S(1)} collective-permute-done((bf16[128,1024]{1,0:T(8,128)(2,1)S(1)}, bf16[128,1024]{1,0:T(8,128)(2,1)S(1)}, u32[]{:S(2)}, u32[]{:S(2)}) %collective-permute-start.27) | collective-permute-done | bytes 262176 | tf_op jit(solution)/shard_map/ppermute | solution.py:36
  197.6 4.2 %shard_map.315 = (bf16[4,64,128]{2,1,0:T(8,128)(2,1)}, f32[128,256]{1,0:T(8,128)}, f32[128,256]{1,0:T(8,128)}, f32[128,256]{1,0:T(8,128)}, f32[128,256]{1,0:T(8,...) custom-call(f32[128,256]{1,0:T(8,128)} %fusion.49.refs_0_.refs_7_, f32[128,256]{1,0:T(8,128)} %fusion.52.refs_1_.refs_8_, ...), custom_call_target="tpu_custom_call" | custom-call | tf_op jit(solution)/shard_map/pallas_call | solution.py:547
  209.3 3.6 collective-permute-done.29.refs_0_
  217.2 3.5 collective-permute-done.31.refs_2_
  224.4 21.8 %shard_map.316 = (bf16[128,256]{1,0:T(8,128)(2,1)}, bf16[128,256]{1,0:T(8,128)(2,1)}, bf16[128,256]{1,0:T(8,128)(2,1)}, bf16[128,256]{1,0:T(8,128)(2,1)}, bf16[1...) custom-call(bf16[4,64,128]{2,1,0:T(8,128)(2,1)} %copy-done.47, ...), custom_call_target="tpu_custom_call" | custom-call | tf_op jit(solution)/shard_map/pallas_call | solution.py:547
  286.6 7.0 %collective-permute-done.39 = f32[1,1024]{1,0:T(1,128)S(1)} collective-permute-done((f32[1,1024]{1,0:T(1,128)}, f32[1,1024]{1,0:T(1,128)S(1)}, u32[]{:S(2)}, u32[]{:S(2)}) %collective-permute-start.39) | collective-permute-done | bytes 4128 | tf_op jit(solution)/shard_map/ppermute | solution.py:826
  296.6 11.9 %all-to-all-start.1 = ((bf16[8,374,128]{2,1,0:T(8,128)(2,1)}), bf16[8,374,128]{2,1,0:T(8,128)(2,1)S(1)}, u32[]{:S(2)}, u32[]{:S(2)}) async-start(bf16[8,374,128]{2,1,0:T(8,128)(2,1)} %pad_add_fusion), calls=%async_computation.1 | async-start | bytes 1540096 | tf_op jit(solution)/shard_map/all_to_all | solution.py:838
  310.7 3.1 fusion
  316.5 27.3 %all-to-all-done.1 = bf16[8,374,128]{2,1,0:T(8,128)(2,1)S(1)} async-done(((bf16[8,374,128]{2,1,0:T(8,128)(2,1)}), bf16[8,374,128]{2,1,0:T(8,128)(2,1)S(1)}, u32[]{:S(2)}, u32[]{:S(2)}) %all-to-all-start.1) | async-done | bytes 765984 | tf_op jit(solution)/shard_map/all_to_all | solution.py:838
  (476 shorter events, 171.1 us)
Async XLA Ops:
  7.2 67.0 %all-gather.12.cloned.1.call-start = ((), (), s32[]{:S(2)}) async-start(), calls=%async_computation.5 | async-start | bytes 2543616 | tf_op jit(solution)/shard_map/all_gather | solution.py:672
  13.6 39.9 %all-to-all-start = ((bf16[8,128,256]{1,2,0:T(8,128)(2,1)}), bf16[8,128,256]{1,2,0:T(8,128)(2,1)S(1)}, u32[]{:S(2)}, u32[]{:S(2)}) async-start(bf16[8,128,256]{1,2,0:T(8,128)(2,1)} %pad_maximum_fusion.1), calls=%async_computation | async-start | bytes 1048576 | tf_op jit(solution)/shard_map/all_to_all | solution.py:680
  20.9 136.9 %all-gather.6.cloned.1.call-start = ((), (), s32[]{:S(2)}) async-start(), calls=%async_computation.2 | async-start | bytes 4718592 | tf_op jit(solution)/shard_map/all_gather | solution.py:712
  23.2 21.5 %collective-permute-start = (bf16[32,377]{1,0:T(8,128)(2,1)S(1)}, bf16[32,377]{1,0:T(8,128)(2,1)S(1)}, u32[]{:S(2)}, u32[]{:S(2)}) collective-permute-start(bf16[32,377]{1,0:T(8,128)(2,1)S(1)} %get-tuple-element.87), channel_id=1, source_target_pairs={{0,4},{4,8},{8,12},{12,16},{16,20},{20,24},{24,28},{28,0},{1,5},{5... | collective-permute-start | bytes 72392 | tf_op jit(solution)/shard_map/ppermute | solution.py:57
  25.3 26.2 %collective-permute-start.1 = (bf16[32,377]{1,0:T(8,128)(2,1)S(1)}, bf16[32,377]{1,0:T(8,128)(2,1)S(1)}, u32[]{:S(2)}, u32[]{:S(2)}) collective-permute-start(bf16[32,377]{1,0:T(8,128)(2,1)S(1)} %get-tuple-element.87), channel_id=1, source_target_pairs={{0,8},{4,12},{8,16},{12,20},{16,24},{20,28},{24,0},{28,4},{1,9},{5... | collective-permute-start | bytes 72392 | tf_op jit(solution)/shard_map/ppermute | solution.py:57
  26.7 26.7 %collective-permute-start.2 = (bf16[32,377]{1,0:T(8,128)(2,1)S(1)}, bf16[32,377]{1,0:T(8,128)(2,1)S(1)}, u32[]{:S(2)}, u32[]{:S(2)}) collective-permute-start(bf16[32,377]{1,0:T(8,128)(2,1)S(1)} %get-tuple-element.87), channel_id=1, source_target_pairs={{0,12},{4,16},{8,20},{12,24},{16,28},{20,0},{24,4},{28,8},{1,13},{... | collective-permute-start | bytes 72392 | tf_op jit(solution)/shard_map/ppermute | solution.py:57
  29.1 26.5 %collective-permute-start.3 = (bf16[32,377]{1,0:T(8,128)(2,1)S(1)}, bf16[32,377]{1,0:T(8,128)(2,1)S(1)}, u32[]{:S(2)}, u32[]{:S(2)}) collective-permute-start(bf16[32,377]{1,0:T(8,128)(2,1)S(1)} %get-tuple-element.87), channel_id=1, source_target_pairs={{0,16},{4,20},{8,24},{12,28},{16,0},{20,4},{24,8},{28,12},{1,17},{... | collective-permute-start | bytes 72392 | tf_op jit(solution)/shard_map/ppermute | solution.py:57
  34.4 21.3 %collective-permute-start.4 = (bf16[32,377]{1,0:T(8,128)(2,1)S(1)}, bf16[32,377]{1,0:T(8,128)(2,1)S(1)}, u32[]{:S(2)}, u32[]{:S(2)}) collective-permute-start(bf16[32,377]{1,0:T(8,128)(2,1)S(1)} %get-tuple-element.87), channel_id=1, source_target_pairs={{0,20},{4,24},{8,28},{12,0},{16,4},{20,8},{24,12},{28,16},{1,21},{... | collective-permute-start | bytes 72392 | tf_op jit(solution)/shard_map/ppermute | solution.py:57
  55.6 205.7 %all-gather.8.cloned.1.call-start = ((), (), s32[]{:S(2)}) async-start(), calls=%async_computation.3 | async-start | bytes 5308416 | tf_op jit(solution)/shard_map/all_gather | solution.py:763
  95.7 12.3 %collective-permute-start.11 = (bf16[4,64,128]{2,1,0:T(8,128)(2,1)}, bf16[4,64,128]{2,1,0:T(8,128)(2,1)S(1)}, u32[]{:S(2)}, u32[]{:S(2)}) collective-permute-start(bf16[4,64,128]{2,1,0:T(8,128)(2,1)} %get-tuple-element.40.refs_13_), channel_id=1, source_target_pairs={{0,28},{1,29},{2,30},{3,31}} | collective-permute-start | bytes 196616 | tf_op jit(solution)/shard_map/ppermute | solution.py:617
  102.0 11.4 %collective-permute-start.13 = (bf16[4,64,128]{2,1,0:T(8,128)(2,1)}, bf16[4,64,128]{2,1,0:T(8,128)(2,1)S(1)}, u32[]{:S(2)}, u32[]{:S(2)}) collective-permute-start(bf16[4,64,128]{2,1,0:T(8,128)(2,1)} %get-tuple-element.40.refs_13_), channel_id=1, source_target_pairs={{0,20},{4,24},{8,28},{1,21},{5,25},{9,29},{2,22},{6,26},{10,30},{3... | collective-permute-start | bytes 196616 | tf_op jit(solution)/shard_map/ppermute | solution.py:617
  124.2 14.1 %collective-permute-start.19 = (bf16[128,1024]{1,0:T(8,128)(2,1)S(1)}, bf16[128,1024]{1,0:T(8,128)(2,1)S(1)}, u32[]{:S(2)}, u32[]{:S(2)}) collective-permute-start(bf16[128,1024]{1,0:T(8,128)(2,1)S(1)} %get-tuple-element.155), channel_id=1, source_target_pairs={{0,2},{1,3},{2,0},{3,1},{4,6},{5,7},{6,4},{7,5},{8,10},{9,11},{10,... | collective-permute-start | bytes 786440 | tf_op jit(solution)/shard_map/ppermute | solution.py:36
  125.8 12.7 %collective-permute-start.18 = (bf16[128,1024]{1,0:T(8,128)(2,1)S(1)}, bf16[128,1024]{1,0:T(8,128)(2,1)S(1)}, u32[]{:S(2)}, u32[]{:S(2)}) collective-permute-start(bf16[128,1024]{1,0:T(8,128)(2,1)S(1)} %get-tuple-element.155), channel_id=1, source_target_pairs={{0,1},{1,2},{2,3},{3,0},{4,5},{5,6},{6,7},{7,4},{8,9},{9,10},{10,1... | collective-permute-start | bytes 786440 | tf_op jit(solution)/shard_map/ppermute | solution.py:36
  163.8 188.4 %all-gather.10.cloned.1.call-start = ((), (), s32[]{:S(2)}) async-start(), calls=%async_computation.4 | async-start | bytes 2506752 | tf_op jit(solution)/shard_map/all_gather | solution.py:802
  172.0 11.2 %collective-permute-start.24 = (bf16[128,256]{1,0:T(8,128)(2,1)S(1)}, bf16[128,256]{1,0:T(8,128)(2,1)S(1)}, u32[]{:S(2)}, u32[]{:S(2)}) collective-permute-start(bf16[128,256]{1,0:T(8,128)(2,1)S(1)} %get-tuple-element.109), channel_id=1, source_target_pairs={{0,3},{1,0},{2,1},{3,2},{4,7},{5,4},{6,5},{7,6},{8,11},{9,8},{10,9... | collective-permute-start | bytes 196616 | tf_op jit(solution)/shard_map/ppermute | solution.py:47
  172.1 11.9 %collective-permute-start.23 = (bf16[128,256]{1,0:T(8,128)(2,1)S(1)}, bf16[128,256]{1,0:T(8,128)(2,1)S(1)}, u32[]{:S(2)}, u32[]{:S(2)}) collective-permute-start(bf16[128,256]{1,0:T(8,128)(2,1)S(1)} %get-tuple-element.110), channel_id=1, source_target_pairs={{0,2},{1,3},{2,0},{3,1},{4,6},{5,7},{6,4},{7,5},{8,10},{9,11},{10,... | collective-permute-start | bytes 196616 | tf_op jit(solution)/shard_map/ppermute | solution.py:47
  182.2 13.4 %collective-permute-start.27 = (bf16[128,1024]{1,0:T(8,128)(2,1)S(1)}, bf16[128,1024]{1,0:T(8,128)(2,1)S(1)}, u32[]{:S(2)}, u32[]{:S(2)}) collective-permute-start(bf16[128,1024]{1,0:T(8,128)(2,1)S(1)} %add_convert_fusion.13), channel_id=1, source_target_pairs={{0,2},{1,3},{2,0},{3,1},{4,6},{5,7},{6,4},{7,5},{8,10},{9,11},{10,... | collective-permute-start | bytes 786440 | tf_op jit(solution)/shard_map/ppermute | solution.py:36
  183.2 12.5 %collective-permute-start.26 = (bf16[128,1024]{1,0:T(8,128)(2,1)S(1)}, bf16[128,1024]{1,0:T(8,128)(2,1)S(1)}, u32[]{:S(2)}, u32[]{:S(2)}) collective-permute-start(bf16[128,1024]{1,0:T(8,128)(2,1)S(1)} %add_convert_fusion.13), channel_id=1, source_target_pairs={{0,1},{1,2},{2,3},{3,0},{4,5},{5,6},{6,7},{7,4},{8,9},{9,10},{10,1... | collective-permute-start | bytes 786440 | tf_op jit(solution)/shard_map/ppermute | solution.py:36
  201.8 11.2 %collective-permute-start.29 = (bf16[4,64,128]{2,1,0:T(8,128)(2,1)}, bf16[4,64,128]{2,1,0:T(8,128)(2,1)S(1)}, u32[]{:S(2)}, u32[]{:S(2)}) collective-permute-start(bf16[4,64,128]{2,1,0:T(8,128)(2,1)} %get-tuple-element.46), channel_id=1, source_target_pairs={{28,0},{29,1},{30,2},{31,3}} | collective-permute-start | bytes 196616 | tf_op jit(solution)/shard_map/ppermute | solution.py:617
  203.1 11.2 %collective-permute-start.30 = (bf16[4,64,128]{2,1,0:T(8,128)(2,1)}, bf16[4,64,128]{2,1,0:T(8,128)(2,1)S(1)}, u32[]{:S(2)}, u32[]{:S(2)}) collective-permute-start(bf16[4,64,128]{2,1,0:T(8,128)(2,1)} %get-tuple-element.46), channel_id=1, source_target_pairs={{24,0},{28,4},{25,1},{29,5},{26,2},{30,6},{27,3},{31,7}} | collective-permute-start | bytes 196616 | tf_op jit(solution)/shard_map/ppermute | solution.py:617
  204.4 16.3 %collective-permute-start.31 = (bf16[4,64,128]{2,1,0:T(8,128)(2,1)}, bf16[4,64,128]{2,1,0:T(8,128)(2,1)S(1)}, u32[]{:S(2)}, u32[]{:S(2)}) collective-permute-start(bf16[4,64,128]{2,1,0:T(8,128)(2,1)} %get-tuple-element.46), channel_id=1, source_target_pairs={{20,0},{24,4},{28,8},{21,1},{25,5},{29,9},{22,2},{26,6},{30,10},{2... | collective-permute-start | bytes 196616 | tf_op jit(solution)/shard_map/ppermute | solution.py:617
  205.7 15.4 %collective-permute-start.32 = (bf16[4,64,128]{2,1,0:T(8,128)(2,1)}, bf16[4,64,128]{2,1,0:T(8,128)(2,1)S(1)}, u32[]{:S(2)}, u32[]{:S(2)}) collective-permute-start(bf16[4,64,128]{2,1,0:T(8,128)(2,1)} %get-tuple-element.46), channel_id=1, source_target_pairs={{16,0},{20,4},{24,8},{28,12},{17,1},{21,5},{25,9},{29,13},{18,2},{... | collective-permute-start | bytes 196616 | tf_op jit(solution)/shard_map/ppermute | solution.py:617
  207.0 14.1 %collective-permute-start.33 = (bf16[4,64,128]{2,1,0:T(8,128)(2,1)}, bf16[4,64,128]{2,1,0:T(8,128)(2,1)S(1)}, u32[]{:S(2)}, u32[]{:S(2)}) collective-permute-start(bf16[4,64,128]{2,1,0:T(8,128)(2,1)} %get-tuple-element.46), channel_id=1, source_target_pairs={{12,0},{16,4},{20,8},{24,12},{28,16},{13,1},{17,5},{21,9},{25,13},... | collective-permute-start | bytes 196616 | tf_op jit(solution)/shard_map/ppermute | solution.py:617
  296.6 47.2 %all-to-all-start.1 = ((bf16[8,374,128]{2,1,0:T(8,128)(2,1)}), bf16[8,374,128]{2,1,0:T(8,128)(2,1)S(1)}, u32[]{:S(2)}, u32[]{:S(2)}) async-start(bf16[8,374,128]{2,1,0:T(8,128)(2,1)} %pad_add_fusion), calls=%async_computation.1 | async-start | bytes 1540096 | tf_op jit(solution)/shard_map/all_to_all | solution.py:838
  (136 other events, 1481.8 us)
Sparse Core Ops, SparseCore 0:
  10.2 64.0 all-gather.11
  76.8 80.9 all-gather.5
  163.9 86.8 all-gather.7
  276.6 70.9 all-gather.9

commit v2 on v1

--- a/solution.py
+++ b/solution.py
@@ -210,6 +210,10 @@
     return dot(xh, yh) + (dot(xh, yl) + dot(xl, yh))
 
 
+def mm1(x, y, dims=NN):
+    return mm(x, y, dims, 1)
+
+
 def cumulate(mask, x, dims=NN):
     ones = mask.astype(F32).astype(BF16)
     high = x.astype(BF16)
@@ -308,7 +312,7 @@
 
 
 def local_kernel(chunk, *refs):
-    tf_ref, rd_ref, ba_ref, sent_ref = refs[RAWS:]
+    tf_ref, rd_ref, ba_ref, sent_ref, saved_ref = refs[RAWS:]
     tokens, width = rd_ref.shape
     geometry = masks(tokens, chunk)
     same, inclusive = (geometry[2], geometry[4])
@@ -330,6 +334,11 @@
         p = head_pieces(ah, rh, bi, ki, vh, geometry, chunk)
         rd_ref[:, lanes] = p["reader"]
         ba_ref[:, lanes] = p["base"]
+        saved_ref[h, :, :tokens] = p["inverse"]
+        saved_ref[h, :, tokens : 2 * tokens] = p["ak"]
+        saved_ref[h, :, 2 * tokens : 4 * tokens] = p["reads"]
+        saved_ref[h, :, 4 * tokens : 4 * tokens + HEAD] = p["u"]
+        saved_ref[h, :, 4 * tokens + HEAD :] = p["w"]
         states = head_states(p, be, ke, vh, scale, chunk)
         total_t = total_f = None
         for c, (transition, fresh) in enumerate(states):
@@ -406,7 +415,7 @@
     got = refs[:count]
     raws = refs[count : count + RAWS]
     (
-        initial_ref, tf_ref, rd_ref, g_ref, recept_ref, key_ref, value_ref,
+        initial_ref, tf_ref, rd_ref, g_ref, saved_ref, recept_ref, key_ref, value_ref,
         dr_ref, dk_ref, dv_ref, ddecay_ref, dlearn_ref, dmix_ref, first_ref, table_ref,
     ) = refs[count + RAWS :]
     tokens, width = rd_ref.shape
@@ -433,8 +442,15 @@
             x[:, lanes] for x in (ah_f, rh_f, bi_f, ki_f, be_f, ke_f, v, scale_f)
         )
         g = g_ref[:, lanes]
-        p = head_pieces(ah, rh, bi, ki, vh, geometry, chunk)
-        u, w = (p["u"], p["w"])
+        p = dict(
+            inverse=saved_ref[h, :, :tokens],
+            ak=saved_ref[h, :, tokens : 2 * tokens],
+            rb=saved_ref[h, :, 2 * tokens : 3 * tokens],
+            reads=saved_ref[h, :, 2 * tokens : 4 * tokens],
+        )
+        u = saved_ref[h, :, 4 * tokens : 4 * tokens + HEAD]
+        w = saved_ref[h, :, 4 * tokens + HEAD :]
+        p["uv"] = jnp.concatenate([u, vh], axis=0)
         starts = [initial_ref[h]]
         for c in range(chunks - 1):
             starts.append(mm(starts[c], tf_ref[h, c, :, :HEAD]) + tf_ref[h, c, :, HEAD:])
@@ -450,12 +466,12 @@
         dw, du, dv, dbe, dke, dreader, dend = ([] for _ in range(7))
         for c in range(chunks):
             s = slice(c * chunk, (c + 1) * chunk)
-            dt = mm(starts[c], nexts[c], TN)
+            dt = mm1(starts[c], nexts[c], TN)
             df = nexts[c]
-            dreader.append(mm(g[s], starts[c]))
-            dw.append(mm(be[s], dt, NT))
-            du.append(mm(be[s], df, NT))
-            dv.append(mm(ke[s], df, NT))
+            dreader.append(mm1(g[s], starts[c]))
+            dw.append(mm1(be[s], dt, NT))
+            du.append(mm1(be[s], df, NT))
+            dv.append(mm1(ke[s], df, NT))
             dbe.append(mm(w[s], dt) + mm(u[s], df))
             dke.append(mm(vh[s], df))
             line = jnp.sum(jnp.where(r64 == c64, dt, 0.0), axis=0, keepdims=True)
@@ -463,18 +479,18 @@
         dw, du, dv, dbe, dke, dreader, dend = (
             jnp.concatenate(x, axis=0) for x in (dw, du, dv, dbe, dke, dreader, dend)
         )
-        dreads = mm(g, p["uv"], NT)
-        drb = jnp.where(inclusive, mm(dreader, w, NT) + dreads[:, :tokens], 0.0)
+        dreads = mm1(g, p["uv"], NT)
+        drb = jnp.where(inclusive, mm1(dreader, w, NT) + dreads[:, :tokens], 0.0)
         drk = jnp.where(inclusive, dreads[:, tokens:], 0.0)
-        duv = mm(p["reads"], g, TN)
-        dw = dw + mm(p["rb"], dreader, TN)
+        duv = mm1(p["reads"], g, TN)
+        dw = dw + mm1(p["rb"], dreader, TN)
         du = du + duv[:tokens]
-        dz = mm(p["inverse"], du, TN)
-        q = mm(p["inverse"], dw, TN)
-        dsolve = mm(dz, p["uv"], NT)
-        dab = jnp.where(strict, mm(q, w, NT) + dsolve[:, :tokens], 0.0)
+        dz = mm1(p["inverse"], du, TN)
+        q = mm1(p["inverse"], dw, TN)
+        dsolve = mm1(dz, p["uv"], NT)
+        dab = jnp.where(strict, mm1(q, w, NT) + dsolve[:, :tokens], 0.0)
         dak = jnp.where(strict, dsolve[:, tokens:], 0.0)
-        dv = dv + duv[tokens:] + mm(p["ak"], dz, TN)
+        dv = dv + duv[tokens:] + mm1(p["ak"], dz, TN)
         dpairs = jnp.concatenate(
             [jnp.concatenate([dab, dak], axis=1), jnp.concatenate([drb, drk], axis=1)], axis=0
         )
@@ -566,6 +582,7 @@
             ((tokens, channels), F32),
             ((tokens, channels), F32),
             ((heads, HEAD, 2 * HEAD), BF16),
+            ((heads, tokens, 4 * tokens + 2 * HEAD), F32),
         ],
     )
 
@@ -597,12 +614,12 @@
     )
 
 
-def wkv_back(got, raws, initial, tf, reader, grad, parts):
+def wkv_back(got, raws, initial, tf, reader, grad, saved, parts):
     tokens, channels = reader.shape
     return wkv_call(
         functools.partial(back_kernel, len(got), chunk_of(tokens)),
         channels,
-        [*got, *raws, initial, tf, reader, grad, *parts],
+        [*got, *raws, initial, tf, reader, grad, saved, *parts],
         [
             *[((tokens, channels), BF16)] * 6,
             ((tokens, channels), F32),
@@ -746,7 +763,7 @@
     raws = (
         key_raw, value_raw, decay_shift, learn_shift, mix_shift, first_value, local_vec, recept
     )
-    states, reader, base, sent = wkv_local(raws)
+    states, reader, base, sent, saved = wkv_local(raws)
     memory_out, pre_out, initial = wkv_outputs(
         state_exchange(sent, 1), raws, states, reader, base, gates
     )
@@ -779,13 +796,17 @@
     )
     grad_gate_up = narrow_tn(gate_sigm, gate_grad)
     gate_low_grad = narrow_nt(gate_grad, gate_up) * gate_sigm * (1.0 - gate_sigm)
+    later = state_exchange(sent_back, -1)
+    shares = stack([share_out(mixed_ffn.astype(BF16)), share_out(middle_grad.astype(BF16))], 1)
+    middle_shared = lax.all_to_all(shares, "seq", split_axis=0, concat_axis=0, tiled=True)
     *row_grads, first_grad, table_param = wkv_back(
-        state_exchange(sent_back, -1),
+        later,
         raws,
         initial,
         states,
         reader,
         memory_grad,
+        saved,
         (recept_part, key_part, value_part),
     )
     decay_shift_grad, learn_shift_grad, mix_shift_grad = row_grads[3:]
@@ -837,8 +858,7 @@
     vec_high, vec_low, _ = split_three(vec_split)
     last = lax.all_to_all(
         stack(
-            [share_out(mixed_ffn.astype(BF16)), share_out(middle_grad.astype(BF16))]
-            + [*second_parts, vec_high, vec_low],
+            [*second_parts, vec_high, vec_low],
             1,
         ),
         "seq",
@@ -846,9 +866,9 @@
         concat_axis=0,
         tiled=True,
     )
-    mixed_all = last[:, :tokens].reshape(seq_size * tokens, share)
-    middle_grad_all = last[:, tokens : 2 * tokens].reshape(seq_size * tokens, share)
-    sums = jnp.sum(last[:, 2 * tokens :].astype(F32), axis=0)
+    mixed_all = middle_shared[:, :tokens].reshape(seq_size * tokens, share)
+    middle_grad_all = middle_shared[:, tokens:].reshape(seq_size * tokens, share)
+    sums = jnp.sum(last.astype(F32), axis=0)
     second_sum = sums[: -2 * columns]
     vec_seq = sums[-2 * columns : -columns] + sums[-columns:]
     vec_mine = head_scatter(vec_seq, F32).T

time: 373 us -> 350 us (0.938)
  Pallas kernels: 45.6 us -> 37 us
  waiting for transfers between devices: 102 us -> 94.6 us
    pallas_call x4, Pallas kernels: 45.6 us -> 37 us  [wkv_call(): pl.pallas_call(kernel, grid=(channels // width,), in_specs=[spec(x.shape)...]
    all_gather x1, waiting for transfers between devices: 0.01 us -> 7.14 us  [body(): final = lax.all_gather(sent_final, 'seq', axis=0, tiled=True)]
    ppermute x1, waiting for transfers between devices: 7.02 us -> 0.01 us  [body(): returned_a = lax.ppermute(prev_a_grad, 'seq', shifted_route('seq', -1))]
    ppermute x14, waiting for transfers between devices: 11.1 us -> 4.3 us  [state_exchange(): lax.ppermute(values, 'seq', shifted_route('seq', distance_sign * distance))]
    all_to_all x1 -> x2, waiting for transfers between devices: 27.3 us -> 22.3 us  [the longest x1 14.4 us: body(): lax.all_to_all(stack([*second_parts, vec_high, vec_low], 1), 'seq', split...]
    all_to_all x1 -> x2, starting transfers between devices: 11.9 us -> 13.4 us  [the longest x1 7.68 us: body(): lax.all_to_all(shares, 'seq', split_axis=0, concat_axis=0, tiled=True)]
  transfers between devices with their start and end apart: 52 -> 53, of which waited for: 24 -> 23; matrix products, arithmetic and copies ran while one was open for 21% -> 22% of each run, Pallas kernels for 12% -> 11%
where the time goes in v2:
time: 350 us; the launch traced here: 347 us
  waiting for transfers between devices  94.6 us (27%)
  starting transfers between devices  86.9 us (25%)
  matrix products  56.8 us (16%)
  Pallas kernels  37 us (11%)
  local copies, waits for them, and re-layouts  28.3 us (8%)
  other arithmetic  26.1 us (7%)
  between operations  17.5 us (5%)
    pallas_call x4, Pallas kernels, wkv_call(): pl.pallas_call(kernel, grid=(channels // width,), in_specs=[spec(x.shape)...  37 us
    dot_general x14, matrix products, narrow_tn(): lax.dot_general(former.astype(BF16), latter.astype(BF16), (((0,), (0,)),...  24.4 us
    ppermute x10, starting transfers between devices, permute_gather(): block = lax.ppermute(rows, axis, ring_route(axis, distance))  24.3 us
    ppermute x14, starting transfers between devices, state_exchange(): lax.ppermute(values, 'seq', shifted_route('seq', distance_sign * distance))  23.9 us
    ppermute x9, waiting for transfers between devices, head_sum(): lax.ppermute(sent, 'head', ring_route('head', distance)).astype(F32)  23.9 us
    dot_general x14, matrix products, narrow_nt(): lax.dot_general(former.astype(BF16), latter.astype(BF16), (((1,), (1,)),...  16.5 us
    dot_general x14, matrix products, narrow_dot(): jnp.dot(former.astype(BF16), latter.astype(BF16), preferred_element_type=...  15.9 us
    all_to_all x1, waiting for transfers between devices, body(): lax.all_to_all(stack([*second_parts, vec_high, vec_low], 1), 'seq', split...  14.4 us
  transfers between devices with their start and end apart: 53, of which 23 were waited for; matrix products, arithmetic and copies ran while one was open for 22% of the time, Pallas kernels for 11%

profile of v2, /device:TPU:0, one launch (start us, length us, event | category | flops | bytes accessed | tf_op | source)
XLA Modules:
  0.0 347.2 jit_solution(4067377656785705922)
XLA Ops:
  13.6 7.3 %all-to-all-start = ((bf16[8,128,256]{1,2,0:T(8,128)(2,1)}), bf16[8,128,256]{1,2,0:T(8,128)(2,1)S(1)}, u32[]{:S(2)}, u32[]{:S(2)}) async-start(bf16[8,128,256]{1,2,0:T(8,128)(2,1)} %pad_maximum_fusion.1), calls=%async_computation | async-start | bytes 1048576 | tf_op jit(solution)/shard_map/all_to_all | solution.py:697
  34.3 5.3 %collective-permute-start.4 = (bf16[32,377]{1,0:T(8,128)(2,1)S(1)}, bf16[32,377]{1,0:T(8,128)(2,1)S(1)}, u32[]{:S(2)}, u32[]{:S(2)}) collective-permute-start(bf16[32,377]{1,0:T(8,128)(2,1)S(1)} %get-tuple-element.89), channel_id=1, source_target_pairs={{0,20},{4,24},{8,28},{12,0},{16,4},{20,8},{24,12},{28,16},{1,21},{... | collective-permute-start | bytes 72392 | tf_op jit(solution)/shard_map/ppermute | solution.py:57
  40.9 3.9 %collective-permute-done = bf16[32,377]{1,0:T(8,128)(2,1)S(1)} collective-permute-done((bf16[32,377]{1,0:T(8,128)(2,1)S(1)}, bf16[32,377]{1,0:T(8,128)(2,1)S(1)}, u32[]{:S(2)}, u32[]{:S(2)}) %collective-permute-start) | collective-permute-done | bytes 24160 | tf_op jit(solution)/shard_map/ppermute | solution.py:57
  44.8 6.7 %collective-permute-start.5 = (bf16[32,377]{1,0:T(8,128)(2,1)S(1)}, bf16[32,377]{1,0:T(8,128)(2,1)S(1)}, u32[]{:S(2)}, u32[]{:S(2)}) collective-permute-start(bf16[32,377]{1,0:T(8,128)(2,1)S(1)} %get-tuple-element.89), channel_id=1, source_target_pairs={{0,24},{4,28},{8,0},{12,4},{16,8},{20,12},{24,16},{28,20},{1,25},{... | collective-permute-start | bytes 72392 | tf_op jit(solution)/shard_map/ppermute | solution.py:57
  61.7 3.5 %collective-permute-done.8 = bf16[256,377]{1,0:T(8,128)(2,1)S(1)} collective-permute-done((bf16[256,377]{1,0:T(8,128)(2,1)S(1)}, bf16[256,377]{1,0:T(8,128)(2,1)S(1)}, u32[]{:S(2)}, u32[]{:S(2)}) %collective-permute-start.8) | collective-permute-done | bytes 193056 | tf_op jit(solution)/shard_map/ppermute | solution.py:57
  70.7 3.6 %all-gather.12.cloned.1.call-done = bf16[4416,256]{1,0:T(8,128)(2,1)} async-done(((bf16[552,256]{1,0:T(8,128)(2,1)}), bf16[4416,256]{1,0:T(8,128)(2,1)}) %all-gather.12.cloned.1.call-update) | async-done | bytes 2261008 | tf_op jit(solution)/shard_map/all_gather | solution.py:689
  84.3 11.8 %shard_map.313 = (f32[4,2,64,128]{3,2,1,0:T(8,128)}, f32[128,256]{1,0:T(8,128)}, f32[128,256]{1,0:T(8,128)}, bf16[4,64,128]{2,1,0:T(8,128)(2,1)}, f32[4,128,640]{2,1,0:T(8,128)}) custom-call(f32[128,256]{1,0:T(8,128)} %fusion.49.refs_0_.refs_7_, f32[128,256]{1,0:T(8,128)} %fusion.52.refs_1_.refs_8_, f32[128,256]{1,0:T(8,128)} %fusion.118.refs_2_.refs_9_, ...), custom_call_target="tpu_custom_call" | custom-call | tf_op jit(solution)/shard_map/pallas_call | solution.py:563
  96.1 4.2 %collective-permute-start.11 = (bf16[4,64,128]{2,1,0:T(8,128)(2,1)}, bf16[4,64,128]{2,1,0:T(8,128)(2,1)S(1)}, u32[]{:S(2)}, u32[]{:S(2)}) collective-permute-start(bf16[4,64,128]{2,1,0:T(8,128)(2,1)} %get-tuple-element.41.refs_13_), channel_id=1, source_target_pairs={{0,28},{1,29},{2,30},{3,31}} | collective-permute-start | bytes 196616 | tf_op jit(solution)/shard_map/ppermute | solution.py:634
  115.3 8.1 %shard_map.314 = (f32[128,256]{1,0:T(8,128)}, bf16[128,256]{1,0:T(8,128)(2,1)}, f32[4,64,64]{2,1,0:T(8,128)}) custom-call(bf16[4,64,128]{2,1,0:T(8,128)(2,1)} %copy-done.54, bf16[4,64,128]{2,1,0:T(8,128)(2,1)} %copy-done.55, bf16[4,64,128]{2,1,0:T(8,128)(2,1)} %copy-done.56, bf16[4,64,128]{2,1,0:T(8,128)(2,1)} %copy-done.57, bf16[4,64,128]{2,1,0:T(8,128)(2,1)} %copy-done.58, ...), custom_call_target="tpu_custom_call" | custom-call | tf_op jit(solution)/shard_map/pallas_call | solution.py:563
  126.3 4.0 %collective-permute-done.20 = bf16[128,1024]{1,0:T(8,128)(2,1)S(1)} collective-permute-done((bf16[128,1024]{1,0:T(8,128)(2,1)S(1)}, bf16[128,1024]{1,0:T(8,128)(2,1)S(1)}, u32[]{:S(2)}, u32[]{:S(2)}) %collective-permute-start.20) | collective-permute-done | bytes 262176 | tf_op jit(solution)/shard_map/ppermute | solution.py:36
  130.3 8.4 %collective-permute-done.19 = bf16[128,1024]{1,0:T(8,128)(2,1)S(1)} collective-permute-done((bf16[128,1024]{1,0:T(8,128)(2,1)S(1)}, bf16[128,1024]{1,0:T(8,128)(2,1)S(1)}, u32[]{:S(2)}, u32[]{:S(2)}) %collective-permute-start.19) | collective-permute-done | bytes 262176 | tf_op jit(solution)/shard_map/ppermute | solution.py:36
  139.5 4.4 %collective-permute-start.21 = (f32[1,1024]{1,0:T(1,128)S(1)}, f32[1,1024]{1,0:T(1,128)S(1)}, u32[]{:S(2)}, u32[]{:S(2)}) collective-permute-start(f32[1,1024]{1,0:T(1,128)S(1)} %slice.412), channel_id=1, source_target_pairs={{0,4},{4,8},{8,12},{12,16},{16,20},{20,24},{24,28},{1,5},{5,9},{9,... | collective-permute-start | bytes 12296 | tf_op jit(solution)/shard_map/ppermute | solution.py:772
  145.3 13.3 %all-gather.6.cloned.1.call-done = bf16[1024,2048]{0,1:T(8,128)(2,1)} async-done(((bf16[128,2048]{0,1:T(8,128)(2,1)}), bf16[1024,2048]{0,1:T(8,128)(2,1)}) %all-gather.6.cloned.1.call-update) | async-done | bytes 4194320 | tf_op jit(solution)/shard_map/all_gather | solution.py:729
  176.8 3.3 collective-permute-done.25
  184.9 4.7 %collective-permute-done.28 = bf16[128,1024]{1,0:T(8,128)(2,1)S(1)} collective-permute-done((bf16[128,1024]{1,0:T(8,128)(2,1)S(1)}, bf16[128,1024]{1,0:T(8,128)(2,1)S(1)}, u32[]{:S(2)}, u32[]{:S(2)}) %collective-permute-start.28) | collective-permute-done | bytes 262176 | tf_op jit(solution)/shard_map/ppermute | solution.py:36
  189.6 6.6 %collective-permute-done.27 = bf16[128,1024]{1,0:T(8,128)(2,1)S(1)} collective-permute-done((bf16[128,1024]{1,0:T(8,128)(2,1)S(1)}, bf16[128,1024]{1,0:T(8,128)(2,1)S(1)}, u32[]{:S(2)}, u32[]{:S(2)}) %collective-permute-start.27) | collective-permute-done | bytes 262176 | tf_op jit(solution)/shard_map/ppermute | solution.py:36
  197.4 4.2 %shard_map.315 = (bf16[4,64,128]{2,1,0:T(8,128)(2,1)}, f32[128,256]{1,0:T(8,128)}, f32[128,256]{1,0:T(8,128)}, f32[128,256]{1,0:T(8,128)}, f32[128,256]{1,0:T(8,...) custom-call(f32[128,256]{1,0:T(8,128)} %fusion.49.refs_0_.refs_7_, f32[128,256]{1,0:T(8,128)} %fusion.52.refs_1_.refs_8_, ...), custom_call_target="tpu_custom_call" | custom-call | tf_op jit(solution)/shard_map/pallas_call | solution.py:563
  216.3 7.7 %all-to-all-start.1 = ((bf16[8,256,128]{2,1,0:T(8,128)(2,1)}), bf16[8,256,128]{2,1,0:T(8,128)(2,1)S(1)}, u32[]{:S(2)}, u32[]{:S(2)}) async-start(bf16[8,256,128]{2,1,0:T(8,128)(2,1)} %pad_add_fusion), calls=%async_computation.1 | async-start | bytes 1048576 | tf_op jit(solution)/shard_map/all_to_all | solution.py:801
  225.5 12.9 %shard_map.316 = (bf16[128,256]{1,0:T(8,128)(2,1)}, bf16[128,256]{1,0:T(8,128)(2,1)}, bf16[128,256]{1,0:T(8,128)(2,1)}, bf16[128,256]{1,0:T(8,128)(2,1)}, bf16[1...) custom-call(bf16[4,64,128]{2,1,0:T(8,128)(2,1)} %copy-done.50, ...), custom_call_target="tpu_custom_call" | custom-call | tf_op jit(solution)/shard_map/pallas_call | solution.py:563
  250.2 7.9 %all-to-all-done.1 = bf16[8,256,128]{2,1,0:T(8,128)(2,1)S(1)} async-done(((bf16[8,256,128]{2,1,0:T(8,128)(2,1)}), bf16[8,256,128]{2,1,0:T(8,128)(2,1)S(1)}, u32[]{:S(2)}, u32[]{:S(2)}) %all-to-all-start.1) | async-done | bytes 524320 | tf_op jit(solution)/shard_map/all_to_all | solution.py:801
  287.1 3.2 fusion
  294.7 5.7 %all-to-all-start.2 = ((bf16[8,118,128]{2,1,0:T(8,128)(2,1)}), bf16[8,118,128]{2,1,0:T(8,128)(2,1)S(1)}, u32[]{:S(2)}, u32[]{:S(2)}) async-start(bf16[8,118,128]{2,1,0:T(8,128)(2,1)} %pad_add_fusion.4), calls=%async_computation.2 | async-start | bytes 491520 | tf_op jit(solution)/shard_map/all_to_all | solution.py:859
  304.0 14.4 %all-to-all-done.2 = bf16[8,118,128]{2,1,0:T(8,128)(2,1)S(1)} async-done(((bf16[8,118,128]{2,1,0:T(8,128)(2,1)}), bf16[8,118,128]{2,1,0:T(8,128)(2,1)S(1)}, u32[]{:S(2)}, u32[]{:S(2)}) %all-to-all-start.2) | async-done | bytes 241696 | tf_op jit(solution)/shard_map/all_to_all | solution.py:859
  323.1 7.1 %all-gather.10.cloned.1.call-done = bf16[1024,1088]{0,1:T(8,128)(2,1)} async-done(((bf16[128,1088]{0,1:T(8,128)(2,1)}), bf16[1024,1088]{0,1:T(8,128)(2,1)}) %all-gather.10.cloned.1.call-update) | async-done | bytes 2228240 | tf_op jit(solution)/shard_map/all_gather | solution.py:823
  (481 shorter events, 167.6 us)
Async XLA Ops:
  7.2 67.0 %all-gather.12.cloned.1.call-start = ((), (), s32[]{:S(2)}) async-start(), calls=%async_computation.6 | async-start | bytes 2543616 | tf_op jit(solution)/shard_map/all_gather | solution.py:689
  13.6 39.9 %all-to-all-start = ((bf16[8,128,256]{1,2,0:T(8,128)(2,1)}), bf16[8,128,256]{1,2,0:T(8,128)(2,1)S(1)}, u32[]{:S(2)}, u32[]{:S(2)}) async-start(bf16[8,128,256]{1,2,0:T(8,128)(2,1)} %pad_maximum_fusion.1), calls=%async_computation | async-start | bytes 1048576 | tf_op jit(solution)/shard_map/all_to_all | solution.py:697
  20.9 137.7 %all-gather.6.cloned.1.call-start = ((), (), s32[]{:S(2)}) async-start(), calls=%async_computation.3 | async-start | bytes 4718592 | tf_op jit(solution)/shard_map/all_gather | solution.py:729
  23.2 21.6 %collective-permute-start = (bf16[32,377]{1,0:T(8,128)(2,1)S(1)}, bf16[32,377]{1,0:T(8,128)(2,1)S(1)}, u32[]{:S(2)}, u32[]{:S(2)}) collective-permute-start(bf16[32,377]{1,0:T(8,128)(2,1)S(1)} %get-tuple-element.89), channel_id=1, source_target_pairs={{0,4},{4,8},{8,12},{12,16},{16,20},{20,24},{24,28},{28,0},{1,5},{5... | collective-permute-start | bytes 72392 | tf_op jit(solution)/shard_map/ppermute | solution.py:57
  25.2 26.2 %collective-permute-start.1 = (bf16[32,377]{1,0:T(8,128)(2,1)S(1)}, bf16[32,377]{1,0:T(8,128)(2,1)S(1)}, u32[]{:S(2)}, u32[]{:S(2)}) collective-permute-start(bf16[32,377]{1,0:T(8,128)(2,1)S(1)} %get-tuple-element.89), channel_id=1, source_target_pairs={{0,8},{4,12},{8,16},{12,20},{16,24},{20,28},{24,0},{28,4},{1,9},{5... | collective-permute-start | bytes 72392 | tf_op jit(solution)/shard_map/ppermute | solution.py:57
  26.7 26.8 %collective-permute-start.2 = (bf16[32,377]{1,0:T(8,128)(2,1)S(1)}, bf16[32,377]{1,0:T(8,128)(2,1)S(1)}, u32[]{:S(2)}, u32[]{:S(2)}) collective-permute-start(bf16[32,377]{1,0:T(8,128)(2,1)S(1)} %get-tuple-element.89), channel_id=1, source_target_pairs={{0,12},{4,16},{8,20},{12,24},{16,28},{20,0},{24,4},{28,8},{1,13},{... | collective-permute-start | bytes 72392 | tf_op jit(solution)/shard_map/ppermute | solution.py:57
  29.0 26.6 %collective-permute-start.3 = (bf16[32,377]{1,0:T(8,128)(2,1)S(1)}, bf16[32,377]{1,0:T(8,128)(2,1)S(1)}, u32[]{:S(2)}, u32[]{:S(2)}) collective-permute-start(bf16[32,377]{1,0:T(8,128)(2,1)S(1)} %get-tuple-element.89), channel_id=1, source_target_pairs={{0,16},{4,20},{8,24},{12,28},{16,0},{20,4},{24,8},{28,12},{1,17},{... | collective-permute-start | bytes 72392 | tf_op jit(solution)/shard_map/ppermute | solution.py:57
  34.3 21.4 %collective-permute-start.4 = (bf16[32,377]{1,0:T(8,128)(2,1)S(1)}, bf16[32,377]{1,0:T(8,128)(2,1)S(1)}, u32[]{:S(2)}, u32[]{:S(2)}) collective-permute-start(bf16[32,377]{1,0:T(8,128)(2,1)S(1)} %get-tuple-element.89), channel_id=1, source_target_pairs={{0,20},{4,24},{8,28},{12,0},{16,4},{20,8},{24,12},{28,16},{1,21},{... | collective-permute-start | bytes 72392 | tf_op jit(solution)/shard_map/ppermute | solution.py:57
  55.6 206.2 %all-gather.8.cloned.1.call-start = ((), (), s32[]{:S(2)}) async-start(), calls=%async_computation.4 | async-start | bytes 5308416 | tf_op jit(solution)/shard_map/all_gather | solution.py:780
  96.1 12.3 %collective-permute-start.11 = (bf16[4,64,128]{2,1,0:T(8,128)(2,1)}, bf16[4,64,128]{2,1,0:T(8,128)(2,1)S(1)}, u32[]{:S(2)}, u32[]{:S(2)}) collective-permute-start(bf16[4,64,128]{2,1,0:T(8,128)(2,1)} %get-tuple-element.41.refs_13_), channel_id=1, source_target_pairs={{0,28},{1,29},{2,30},{3,31}} | collective-permute-start | bytes 196616 | tf_op jit(solution)/shard_map/ppermute | solution.py:634
  102.3 11.4 %collective-permute-start.13 = (bf16[4,64,128]{2,1,0:T(8,128)(2,1)}, bf16[4,64,128]{2,1,0:T(8,128)(2,1)S(1)}, u32[]{:S(2)}, u32[]{:S(2)}) collective-permute-start(bf16[4,64,128]{2,1,0:T(8,128)(2,1)} %get-tuple-element.41.refs_13_), channel_id=1, source_target_pairs={{0,20},{4,24},{8,28},{1,21},{5,25},{9,29},{2,22},{6,26},{10,30},{3... | collective-permute-start | bytes 196616 | tf_op jit(solution)/shard_map/ppermute | solution.py:634
  124.6 14.1 %collective-permute-start.19 = (bf16[128,1024]{1,0:T(8,128)(2,1)S(1)}, bf16[128,1024]{1,0:T(8,128)(2,1)S(1)}, u32[]{:S(2)}, u32[]{:S(2)}) collective-permute-start(bf16[128,1024]{1,0:T(8,128)(2,1)S(1)} %get-tuple-element.157), channel_id=1, source_target_pairs={{0,2},{1,3},{2,0},{3,1},{4,6},{5,7},{6,4},{7,5},{8,10},{9,11},{10,... | collective-permute-start | bytes 786440 | tf_op jit(solution)/shard_map/ppermute | solution.py:36
  126.2 12.7 %collective-permute-start.18 = (bf16[128,1024]{1,0:T(8,128)(2,1)S(1)}, bf16[128,1024]{1,0:T(8,128)(2,1)S(1)}, u32[]{:S(2)}, u32[]{:S(2)}) collective-permute-start(bf16[128,1024]{1,0:T(8,128)(2,1)S(1)} %get-tuple-element.157), channel_id=1, source_target_pairs={{0,1},{1,2},{2,3},{3,0},{4,5},{5,6},{6,7},{7,4},{8,9},{9,10},{10,1... | collective-permute-start | bytes 786440 | tf_op jit(solution)/shard_map/ppermute | solution.py:36
  173.0 11.2 %collective-permute-start.23 = (bf16[128,256]{1,0:T(8,128)(2,1)S(1)}, bf16[128,256]{1,0:T(8,128)(2,1)S(1)}, u32[]{:S(2)}, u32[]{:S(2)}) collective-permute-start(bf16[128,256]{1,0:T(8,128)(2,1)S(1)} %get-tuple-element.112), channel_id=1, source_target_pairs={{0,2},{1,3},{2,0},{3,1},{4,6},{5,7},{6,4},{7,5},{8,10},{9,11},{10,... | collective-permute-start | bytes 196616 | tf_op jit(solution)/shard_map/ppermute | solution.py:47
  182.9 13.3 %collective-permute-start.27 = (bf16[128,1024]{1,0:T(8,128)(2,1)S(1)}, bf16[128,1024]{1,0:T(8,128)(2,1)S(1)}, u32[]{:S(2)}, u32[]{:S(2)}) collective-permute-start(bf16[128,1024]{1,0:T(8,128)(2,1)S(1)} %add_convert_fusion.13), channel_id=1, source_target_pairs={{0,2},{1,3},{2,0},{3,1},{4,6},{5,7},{6,4},{7,5},{8,10},{9,11},{10,... | collective-permute-start | bytes 786440 | tf_op jit(solution)/shard_map/ppermute | solution.py:36
  183.4 12.8 %collective-permute-start.26 = (bf16[128,1024]{1,0:T(8,128)(2,1)S(1)}, bf16[128,1024]{1,0:T(8,128)(2,1)S(1)}, u32[]{:S(2)}, u32[]{:S(2)}) collective-permute-start(bf16[128,1024]{1,0:T(8,128)(2,1)S(1)} %add_convert_fusion.13), channel_id=1, source_target_pairs={{0,1},{1,2},{2,3},{3,0},{4,5},{5,6},{6,7},{7,4},{8,9},{9,10},{10,1... | collective-permute-start | bytes 786440 | tf_op jit(solution)/shard_map/ppermute | solution.py:36
  201.7 11.2 %collective-permute-start.29 = (bf16[4,64,128]{2,1,0:T(8,128)(2,1)}, bf16[4,64,128]{2,1,0:T(8,128)(2,1)S(1)}, u32[]{:S(2)}, u32[]{:S(2)}) collective-permute-start(bf16[4,64,128]{2,1,0:T(8,128)(2,1)} %get-tuple-element.47), channel_id=1, source_target_pairs={{28,0},{29,1},{30,2},{31,3}} | collective-permute-start | bytes 196616 | tf_op jit(solution)/shard_map/ppermute | solution.py:634
  204.3 19.8 %collective-permute-start.31 = (bf16[4,64,128]{2,1,0:T(8,128)(2,1)}, bf16[4,64,128]{2,1,0:T(8,128)(2,1)}, u32[]{:S(2)}, u32[]{:S(2)}) collective-permute-start(bf16[4,64,128]{2,1,0:T(8,128)(2,1)} %get-tuple-element.47), channel_id=1, source_target_pairs={{20,0},{24,4},{28,8},{21,1},{25,5},{29,9},{22,2},{26,6},{30,10},{2... | collective-permute-start | bytes 196616 | tf_op jit(solution)/shard_map/ppermute | solution.py:634
  205.6 18.5 %collective-permute-start.32 = (bf16[4,64,128]{2,1,0:T(8,128)(2,1)}, bf16[4,64,128]{2,1,0:T(8,128)(2,1)}, u32[]{:S(2)}, u32[]{:S(2)}) collective-permute-start(bf16[4,64,128]{2,1,0:T(8,128)(2,1)} %get-tuple-element.47), channel_id=1, source_target_pairs={{16,0},{20,4},{24,8},{28,12},{17,1},{21,5},{25,9},{29,13},{18,2},{... | collective-permute-start | bytes 196616 | tf_op jit(solution)/shard_map/ppermute | solution.py:634
  206.9 17.2 %collective-permute-start.33 = (bf16[4,64,128]{2,1,0:T(8,128)(2,1)}, bf16[4,64,128]{2,1,0:T(8,128)(2,1)}, u32[]{:S(2)}, u32[]{:S(2)}) collective-permute-start(bf16[4,64,128]{2,1,0:T(8,128)(2,1)} %get-tuple-element.47), channel_id=1, source_target_pairs={{12,0},{16,4},{20,8},{24,12},{28,16},{13,1},{17,5},{21,9},{25,13},... | collective-permute-start | bytes 196616 | tf_op jit(solution)/shard_map/ppermute | solution.py:634
  212.8 12.0 %collective-permute-start.34 = (bf16[4,64,128]{2,1,0:T(8,128)(2,1)}, bf16[4,64,128]{2,1,0:T(8,128)(2,1)S(1)}, u32[]{:S(2)}, u32[]{:S(2)}) collective-permute-start(bf16[4,64,128]{2,1,0:T(8,128)(2,1)} %get-tuple-element.47), channel_id=1, source_target_pairs={{8,0},{12,4},{16,8},{20,12},{24,16},{28,20},{9,1},{13,5},{17,9},{2... | collective-permute-start | bytes 196616 | tf_op jit(solution)/shard_map/ppermute | solution.py:634
  216.3 41.8 %all-to-all-start.1 = ((bf16[8,256,128]{2,1,0:T(8,128)(2,1)}), bf16[8,256,128]{2,1,0:T(8,128)(2,1)S(1)}, u32[]{:S(2)}, u32[]{:S(2)}) async-start(bf16[8,256,128]{2,1,0:T(8,128)(2,1)} %pad_add_fusion), calls=%async_computation.1 | async-start | bytes 1048576 | tf_op jit(solution)/shard_map/all_to_all | solution.py:801
  224.0 106.2 %all-gather.10.cloned.1.call-start = ((), (), s32[]{:S(2)}) async-start(), calls=%async_computation.5 | async-start | bytes 2506752 | tf_op jit(solution)/shard_map/all_gather | solution.py:823
  294.7 23.8 %all-to-all-start.2 = ((bf16[8,118,128]{2,1,0:T(8,128)(2,1)}), bf16[8,118,128]{2,1,0:T(8,128)(2,1)S(1)}, u32[]{:S(2)}, u32[]{:S(2)}) async-start(bf16[8,118,128]{2,1,0:T(8,128)(2,1)} %pad_add_fusion.4), calls=%async_computation.2 | async-start | bytes 491520 | tf_op jit(solution)/shard_map/all_to_all | solution.py:859
  (138 other events, 1411.7 us)
Sparse Core Ops, SparseCore 0:
  10.2 63.9 all-gather.11
  76.8 81.7 all-gather.5
  164.7 97.1 all-gather.7
  275.0 55.1 all-gather.9
